TPU v7x, 32 devices: a whole 2x2x4 slice. The times are simulated.
32 devices in a mesh: fsdp: 8 (over z, x), context: 4 (over y, core).
Axes of the slice: x: 2, y: 2, z: 4, core: 2. Of those that a mesh axis runs over, the one named last changes fastest.
Arguments:
- tokens: bfloat16 [16, 1024, 1536], P('fsdp', 'context'), may hold values from -6 to 6
- segments: int32 [16, 1024], P('fsdp', 'context'), may hold values from 0 to 15, never falling along the last dimension, each value on 1 to 512 neighbouring positions
- w_query: bfloat16 [1536, 1536], P('fsdp'), may hold values from -0.15625 to 0.15625
- w_key: bfloat16 [1536, 768], P('fsdp'), may hold values from -0.15625 to 0.15625
- w_value: bfloat16 [1536, 768], P('fsdp'), may hold values from -0.15625 to 0.15625
- w_out: bfloat16 [1536, 1536], P('fsdp'), may hold values from -0.875 to 0.875
- w_gate: bfloat16 [1536, 4096], P('fsdp', 'context'), may hold values from -0.15625 to 0.15625
- w_up: bfloat16 [1536, 4096], P('fsdp', 'context'), may hold values from -0.15625 to 0.15625
- w_down: bfloat16 [4096, 1536], P('context', 'fsdp'), may hold values from -0.09375 to 0.09375
- gain_attn: bfloat16 [1536], P('fsdp'), may hold values from 0.5 to 1.5
- gain_mlp: bfloat16 [1536], P('fsdp'), may hold values from 0.5 to 1.5
- cotangent: bfloat16 [16, 1024, 1536], P('fsdp', 'context'), may hold values from -6 to 6
Outputs:
- output: bfloat16 [16, 1024, 1536], P('fsdp', 'context')
- grad_tokens: float32 [16, 1024, 1536], P('fsdp', 'context')
- grad_w_query: float32 [1536, 1536], P('fsdp')
- grad_w_key: float32 [1536, 768], P('fsdp')
- grad_w_value: float32 [1536, 768], P('fsdp')
- grad_w_out: float32 [1536, 1536], P('fsdp')
- grad_w_gate: float32 [1536, 4096], P('fsdp', 'context')
- grad_w_up: float32 [1536, 4096], P('fsdp', 'context')
- grad_w_down: float32 [4096, 1536], P('context', 'fsdp')
- grad_gain_attn: float32 [1536], P('fsdp')
- grad_gain_mlp: float32 [1536], P('fsdp')
Inputs may be any that keep to these rules, and one draw needn't show every extreme that they name: `segments`: in each sequence segment numbers never fall and all 16 documents appear; the longest has exactly 512 tokens.
All inputs are finite; a program needn't handle non-finite values.
Results may differ from a plain program's by a relative error of at most 0.02.
Values may be sent and summed in bfloat16 or wider, within the bound.
No kernel may reach another device: no remote copies, remote signals or barrier semaphores. Data moves between devices by JAX's collectives and lax.ppermute only.
A program may use at most 256 MiB of HBM per device.

v0:
```python
import math

import jax
import jax.numpy as jnp
from jax import lax
from jax.sharding import PartitionSpec as P

H = 16
KVH = 8
HD = 96


EPSILON = 1e-05
THETA = 100000.0


def rms_scale(values, gain):
    return values * lax.rsqrt(jnp.mean(values * values, axis=-1, keepdims=True) + EPSILON) * gain


def rotate(values, cosines, sines):
    half_width = values.shape[-1] // 2
    leading = values[..., :half_width]
    trailing = values[..., half_width:]
    return jnp.concatenate(
        [leading * cosines - trailing * sines, trailing * cosines + leading * sines], axis=-1
    )


def gated(gate_act, up_act):
    return jax.nn.silu(gate_act) * up_act


def inner(left, right):
    return jnp.einsum("ti,tj->ij", left, right, preferred_element_type=jnp.float32)


def outer_back(grad_rows, weight):
    return jnp.einsum("ti,ji->tj", grad_rows, weight, preferred_element_type=jnp.float32)


def reduce_grads(parts):
    shares = (
        lax.psum_scatter(
            parts[0].astype(jnp.bfloat16), "fsdp", scatter_dimension=0, tiled=True
        ).astype(jnp.float32),
        lax.psum_scatter(
            parts[1].astype(jnp.bfloat16), "fsdp", scatter_dimension=0, tiled=True
        ).astype(jnp.float32),
        lax.psum_scatter(
            parts[2].astype(jnp.bfloat16), "fsdp", scatter_dimension=0, tiled=True
        ).astype(jnp.float32),
        lax.psum_scatter(
            parts[3].astype(jnp.bfloat16), "fsdp", scatter_dimension=0, tiled=True
        ).astype(jnp.float32),
        lax.psum_scatter(
            parts[4].astype(jnp.bfloat16), "fsdp", scatter_dimension=0, tiled=True
        ).astype(jnp.float32),
        lax.psum_scatter(
            parts[5].astype(jnp.bfloat16), "fsdp", scatter_dimension=0, tiled=True
        ).astype(jnp.float32),
    )
    result = (
        lax.psum(shares[0].astype(jnp.bfloat16), "context").astype(jnp.float32),
        lax.psum(shares[1].astype(jnp.bfloat16), "context").astype(jnp.float32),
        lax.psum(shares[2].astype(jnp.bfloat16), "context").astype(jnp.float32),
        lax.psum(shares[3].astype(jnp.bfloat16), "context").astype(jnp.float32),
        lax.psum(shares[4].astype(jnp.bfloat16), "context").astype(jnp.float32),
        lax.psum(shares[5].astype(jnp.bfloat16), "context").astype(jnp.float32),
    )
    return result


def gather_attention(shard_query, shard_key, shard_value, shard_out, shard_gain_a, shard_gain_m):
    return (
        lax.all_gather(shard_query, "fsdp", axis=0, tiled=True),
        lax.all_gather(shard_key, "fsdp", axis=0, tiled=True),
        lax.all_gather(shard_value, "fsdp", axis=0, tiled=True),
        lax.all_gather(shard_out, "fsdp", axis=0, tiled=True),
        lax.all_gather(shard_gain_a, "fsdp", axis=0, tiled=True),
        lax.all_gather(shard_gain_m, "fsdp", axis=0, tiled=True),
    )


def gather_mlp(shard_gate, shard_up, shard_down):
    return (
        lax.all_gather(shard_gate, "fsdp", axis=0, tiled=True),
        lax.all_gather(shard_up, "fsdp", axis=0, tiled=True),
        lax.all_gather(shard_down, "fsdp", axis=1, tiled=True),
    )


def on_device(
    tokens,
    segments,
    w_query,
    w_key,
    w_value,
    w_out,
    w_gate,
    w_up,
    w_down,
    gain_attn,
    gain_mlp,
    cotangent,
):
    seq_count, tok_local, model_width = tokens.shape
    row_count = seq_count * tok_local
    groups = H // KVH
    kv_width = KVH * HD
    logit_scale = 1.0 / math.sqrt(HD)
    whole_seg = lax.all_gather(segments, "context", axis=1, tiled=True)
    length = whole_seg.shape[1]
    all_rows = seq_count * length
    offset = lax.axis_index("context") * tok_local
    key_index = jnp.arange(length, dtype=jnp.int32)
    query_index = offset + jnp.arange(tok_local, dtype=jnp.int32)
    starts = jnp.concatenate(
        [jnp.ones((seq_count, 1), dtype=bool), whole_seg[:, 1:] != whole_seg[:, :-1]], axis=1
    )
    first_index = lax.cummax(jnp.where(starts, key_index[None, :], 0), axis=1)
    positions = lax.dynamic_slice_in_dim(key_index[None, :] - first_index, offset, tok_local, 1)
    frequency = jnp.power(THETA, -(jnp.arange(HD // 2, dtype=jnp.float32) * 2.0 / HD))
    angles = positions.astype(jnp.float32)[:, :, None] * frequency[None, None, :]
    cosines = jnp.cos(angles).reshape(row_count, 1, HD // 2)
    sines = jnp.sin(angles).reshape(row_count, 1, HD // 2)
    x_flat = tokens.reshape(row_count, model_width).astype(jnp.float32)

    def masked_scores(query_sequence, k_seq, q_seg, k_seg):
        unscaled_scores = (
            jnp.einsum(
                "wxif,axf->xiwa",
                query_sequence,
                k_seq.reshape(length, KVH, HD),
                preferred_element_type=jnp.float32,
            )
            * logit_scale
        )
        allowed = (q_seg[:, None] == k_seg[None, :]) & (key_index[None, :] <= query_index[:, None])
        return jnp.where(allowed[None, None], unscaled_scores, -1e30)

    def attend(items):
        query_sequence, k_seq, v_seq, q_seg, k_seg = items
        scores = masked_scores(query_sequence, k_seq, q_seg, k_seg)
        top_score = jnp.max(scores, axis=-1, keepdims=True)
        weights = jnp.exp(scores - top_score)
        total = jnp.sum(weights, axis=-1, keepdims=True)
        attention_probabilities = (weights / total).astype(jnp.bfloat16)
        mixed_seq = jnp.einsum(
            "uvqe,eua->quva",
            attention_probabilities,
            v_seq.reshape(length, KVH, HD),
            preferred_element_type=jnp.float32,
        ).astype(jnp.bfloat16)
        return (mixed_seq, top_score + jnp.log(total))

    def forward(attn_weights, mlp_weights):
        full_query, full_key, full_value, full_out, full_gain_a, full_gain_m = attn_weights
        normed = rms_scale(x_flat, full_gain_a.astype(jnp.float32)).astype(jnp.bfloat16)
        queries = jnp.dot(normed, full_query, preferred_element_type=jnp.float32).reshape(
            row_count, H, HD
        )
        key_rows = jnp.dot(normed, full_key, preferred_element_type=jnp.float32).reshape(
            row_count, KVH, HD
        )
        value_matrix_rows = jnp.dot(normed, full_value, preferred_element_type=jnp.float32).astype(
            jnp.bfloat16
        )
        qrot = (
            rotate(queries, cosines, sines)
            .astype(jnp.bfloat16)
            .reshape(seq_count, tok_local, KVH, groups, HD)
        )
        rotary_keys = (
            rotate(key_rows, cosines, sines)
            .astype(jnp.bfloat16)
            .reshape(seq_count, tok_local, kv_width)
        )
        all_keys, all_values = (
            lax.all_gather(rotary_keys, "context", axis=1, tiled=True),
            lax.all_gather(
                value_matrix_rows.reshape(seq_count, tok_local, kv_width),
                "context",
                axis=1,
                tiled=True,
            ),
        )
        mixed, log_totals = lax.map(attend, (qrot, all_keys, all_values, segments, whole_seg))
        mixed_flat = mixed.reshape(row_count, H * HD)
        resid = x_flat + jnp.dot(mixed_flat, full_out, preferred_element_type=jnp.float32)
        full_gate, full_up, full_down = mlp_weights
        normed_two = rms_scale(resid, full_gain_m.astype(jnp.float32)).astype(jnp.bfloat16)
        all_normed_two = lax.all_gather(
            normed_two.reshape(seq_count, tok_local, model_width), "context", axis=1, tiled=True
        ).reshape(all_rows, model_width)
        gate_act = jnp.dot(all_normed_two, full_gate, preferred_element_type=jnp.float32)
        up_act = jnp.dot(all_normed_two, full_up, preferred_element_type=jnp.float32)
        hidden = gated(gate_act, up_act).astype(jnp.bfloat16)
        partial_down = jnp.dot(hidden, full_down, preferred_element_type=jnp.float32)
        down_sum = (
            lax.psum_scatter(
                partial_down.reshape(seq_count, length, model_width).astype(jnp.bfloat16),
                "context",
                scatter_dimension=1,
                tiled=True,
            )
            .astype(jnp.float32)
            .reshape(row_count, model_width)
        )
        final = resid + down_sum
        return (
            final,
            normed,
            qrot,
            all_keys,
            all_values,
            mixed,
            log_totals,
            resid,
            all_normed_two,
            gate_act,
            up_act,
            hidden,
        )

    attn_weights = gather_attention(w_query, w_key, w_value, w_out, gain_attn, gain_mlp)
    mlp_weights = gather_mlp(w_gate, w_up, w_down)
    state = forward(attn_weights, mlp_weights)
    output = state[0].astype(jnp.bfloat16).reshape(seq_count, tok_local, model_width)
    fresh = lax.optimization_barrier(
        (w_query, w_key, w_value, w_out, gain_attn, gain_mlp, w_gate, w_up, w_down, output)
    )
    attn_weights = gather_attention(fresh[0], fresh[1], fresh[2], fresh[3], fresh[4], fresh[5])
    mlp_weights = gather_mlp(fresh[6], fresh[7], fresh[8])
    state = forward(attn_weights, mlp_weights)
    (
        final,
        normed,
        qrot,
        all_keys,
        all_values,
        mixed,
        log_totals,
        resid,
        all_normed_two,
        gate_act,
        up_act,
        hidden,
    ) = state
    full_query, full_key, full_value, full_out, full_gain_a, full_gain_m = attn_weights
    full_gate, full_up, full_down = mlp_weights
    grad_out = cotangent.reshape(row_count, model_width)
    all_grad_out = lax.all_gather(cotangent, "context", axis=1, tiled=True).reshape(
        all_rows, model_width
    )
    grad_down_t = inner(all_grad_out, hidden)
    grad_hidden = outer_back(all_grad_out, full_down)
    gate_pull = jax.vjp(gated, gate_act, up_act)[1]
    grad_gate_f, grad_up_f = gate_pull(grad_hidden)
    grad_gate_act = grad_gate_f.astype(jnp.bfloat16)
    grad_up_act = grad_up_f.astype(jnp.bfloat16)
    grad_gate = inner(all_normed_two, grad_gate_act)
    grad_up = inner(all_normed_two, grad_up_act)
    part_normed_two = outer_back(grad_gate_act, full_gate) + outer_back(grad_up_act, full_up)
    grad_normed_two = lax.psum_scatter(
        part_normed_two.reshape(seq_count, length, model_width),
        "context",
        scatter_dimension=1,
        tiled=True,
    ).reshape(row_count, model_width)
    norm_pull = jax.vjp(rms_scale, resid, full_gain_m.astype(jnp.float32))[1]
    back_resid, grad_gain_m = norm_pull(grad_normed_two)
    mlp_shares = (
        lax.psum_scatter(
            grad_gate.astype(jnp.bfloat16), "fsdp", scatter_dimension=0, tiled=True
        ).astype(jnp.float32),
        lax.psum_scatter(
            grad_up.astype(jnp.bfloat16), "fsdp", scatter_dimension=0, tiled=True
        ).astype(jnp.float32),
        lax.psum_scatter(
            grad_down_t.astype(jnp.bfloat16), "fsdp", scatter_dimension=0, tiled=True
        ).astype(jnp.float32),
    )
    grad_resid = grad_out.astype(jnp.float32) + back_resid
    grad_attn = grad_resid.astype(jnp.bfloat16)
    mixed_flat = mixed.reshape(row_count, H * HD)
    grad_out_w = inner(mixed_flat, grad_attn)
    grad_mixed = (
        outer_back(grad_attn, full_out)
        .astype(jnp.bfloat16)
        .reshape(seq_count, tok_local, KVH, groups, HD)
    )

    def attend_back(items):
        query_sequence, k_seq, v_seq, q_seg, k_seg, log_total, grad_seq = items
        scores = masked_scores(query_sequence, k_seq, q_seg, k_seg)
        attention_probabilities = jnp.exp(scores - log_total)
        grad_probs = jnp.einsum(
            "wxif,axf->xiwa",
            grad_seq,
            v_seq.reshape(length, KVH, HD),
            preferred_element_type=jnp.float32,
        )
        weighted = jnp.sum(attention_probabilities * grad_probs, axis=-1, keepdims=True)
        score_gradient = (attention_probabilities * (grad_probs - weighted)).astype(jnp.bfloat16)
        grad_q = (
            jnp.einsum(
                "uvqe,eua->quva",
                score_gradient,
                k_seq.reshape(length, KVH, HD),
                preferred_element_type=jnp.float32,
            )
            * logit_scale
        )
        grad_k = (
            jnp.einsum(
                "jnbp,bjny->pjy", score_gradient, query_sequence, preferred_element_type=jnp.float32
            )
            * logit_scale
        )
        grad_v = jnp.einsum(
            "jnbp,bjny->pjy",
            attention_probabilities.astype(jnp.bfloat16),
            grad_seq,
            preferred_element_type=jnp.float32,
        )
        return (grad_q, grad_k.reshape(length, kv_width), grad_v.reshape(length, kv_width))

    grad_qrot, part_keys, part_values = lax.map(
        attend_back, (qrot, all_keys, all_values, segments, whole_seg, log_totals, grad_mixed)
    )
    grad_krot, grad_vals = (
        lax.psum_scatter(
            part_keys.astype(jnp.bfloat16), "context", scatter_dimension=1, tiled=True
        ).astype(jnp.float32),
        lax.psum_scatter(
            part_values.astype(jnp.bfloat16), "context", scatter_dimension=1, tiled=True
        ).astype(jnp.float32),
    )
    grad_queries = (
        rotate(grad_qrot.reshape(row_count, H, HD), cosines, -sines)
        .astype(jnp.bfloat16)
        .reshape(row_count, H * HD)
    )
    grad_keys = (
        rotate(grad_krot.reshape(row_count, KVH, HD), cosines, -sines)
        .astype(jnp.bfloat16)
        .reshape(row_count, kv_width)
    )
    grad_values = grad_vals.reshape(row_count, kv_width).astype(jnp.bfloat16)
    grad_query_w = inner(normed, grad_queries)
    grad_key_w = inner(normed, grad_keys)
    grad_value_w = inner(normed, grad_values)
    grad_normed = (
        outer_back(grad_queries, full_query)
        + outer_back(grad_keys, full_key)
        + outer_back(grad_values, full_value)
    )
    first_pull = jax.vjp(rms_scale, x_flat, full_gain_a.astype(jnp.float32))[1]
    back_input, grad_gain_a = first_pull(grad_normed)
    attn_grads = reduce_grads(
        (grad_query_w, grad_key_w, grad_value_w, grad_out_w, grad_gain_a, grad_gain_m)
    )
    grad_input = (grad_resid + back_input).reshape(seq_count, tok_local, model_width)
    return (
        output,
        grad_input,
        attn_grads[0],
        attn_grads[1],
        attn_grads[2],
        attn_grads[3],
        mlp_shares[0],
        mlp_shares[1],
        jnp.transpose(mlp_shares[2]),
        attn_grads[4],
        attn_grads[5],
    )


def solution(mesh):
    return jax.shard_map(
        on_device,
        mesh=mesh,
        in_specs=(
            P("fsdp", "context", None),
            P("fsdp", "context"),
            P("fsdp", None),
            P("fsdp", None),
            P("fsdp", None),
            P("fsdp", None),
            P("fsdp", "context"),
            P("fsdp", "context"),
            P("context", "fsdp"),
            P("fsdp"),
            P("fsdp"),
            P("fsdp", "context", None),
        ),
        out_specs=(
            P("fsdp", "context", None),
            P("fsdp", "context", None),
            P("fsdp", None),
            P("fsdp", None),
            P("fsdp", None),
            P("fsdp", None),
            P("fsdp", "context"),
            P("fsdp", "context"),
            P("context", "fsdp"),
            P("fsdp"),
            P("fsdp"),
        ),
        check_vma=False,
    )
```

profile of v0, /device:TPU:1, one launch (start us, length us, event | category | flops | bytes accessed | tf_op | source)
XLA Modules:
  0.0 2306.1 jit_solution(10528098979458675509)
XLA Ops:
  73.3 43.1 %all-gather.22.cloned.1.call-done = bf16[1536,768]{1,0:T(8,128)(2,1)} async-done(((bf16[192,768]{1,0:T(8,128)(2,1)}), bf16[1536,768]{1,0:T(8,128)(2,1)}) %all-gather.22.cloned.1.call-update) | async-done | bytes 2359312 | tf_op jit(solution)/shard_map/all_gather | solution.py:78
  123.0 74.3 %all-gather.30.cloned.1.call-done = bf16[1536,1536]{1,0:T(8,128)(2,1)} async-done(((bf16[192,1536]{1,0:T(8,128)(2,1)}), bf16[1536,1536]{1,0:T(8,128)(2,1)}) %all-gather.30.cloned.1.call-update) | async-done | bytes 4718608 | tf_op jit(solution)/shard_map/all_gather | solution.py:76
  227.8 30.9 %all-gather.24.cloned.1.call-done = bf16[2,1024,768]{1,2,0:T(8,128)(2,1)} async-done(((bf16[2,256,768]{1,2,0:T(8,128)(2,1)}), bf16[2,1024,768]{1,2,0:T(8,128)(2,1)}) %all-gather.24.cloned.1.call-update) | async-done | bytes 3145744 | tf_op jit(solution)/shard_map/all_gather | solution.py:181
  260.1 43.3 %while.39 = (s32[]{:T(128)}, bf16[2,256,8,2,96]{1,4,3,2,0:T(8,128)(2,1)}, bf16[2,1024,768]{1,2,0:T(8,128)(2,1)}, s32[2,256]{1,0:T(2,128)S(1)}, s32[2,1024]{1,0:T...) while((s32[]{:T(128)}, ...), condition=%wide.region_6.7_spmd.clone, body=%wide.region_3.6_spmd.clone.sunk | while | flops 1636959488 | bytes 45139068 | solution.py:188
  306.9 32.4 %all-gather.32.cloned.1.call-done = bf16[1536,1536]{1,0:T(8,128)(2,1)} async-done(((bf16[192,1536]{1,0:T(8,128)(2,1)}), bf16[1536,1536]{1,0:T(8,128)(2,1)}) %all-gather.32.cloned.1.call-update) | async-done | bytes 4718608 | tf_op jit(solution)/shard_map/all_gather | solution.py:79
  349.2 51.1 %all-gather.36.cloned.1.call-done = bf16[1536,1024]{1,0:T(8,128)(2,1)} async-done(((bf16[192,1024]{1,0:T(8,128)(2,1)}), bf16[1536,1024]{1,0:T(8,128)(2,1)}) %all-gather.36.cloned.1.call-update) | async-done | bytes 3145744 | tf_op jit(solution)/shard_map/all_gather | solution.py:87
  400.2 48.4 %all-gather.34.cloned.1.call-done = bf16[2,1024,1536]{2,1,0:T(8,128)(2,1)} async-done(((bf16[2,256,1536]{2,1,0:T(8,128)(2,1)}), bf16[2,1024,1536]{2,1,0:T(8,128)(2,1)}) %all-gather.34.cloned.1.call-update) | async-done | bytes 6291472 | tf_op jit(solution)/shard_map/all_gather | solution.py:193
  460.4 49.7 %all-gather.38.cloned.1.call-done = bf16[1536,1024]{1,0:T(8,128)(2,1)} async-done(((bf16[192,1024]{1,0:T(8,128)(2,1)}), bf16[1536,1024]{1,0:T(8,128)(2,1)}) %all-gather.38.cloned.1.call-update) | async-done | bytes 3145744 | tf_op jit(solution)/shard_map/all_gather | solution.py:88
  510.1 61.1 %all-gather.40.cloned.1.call-done = bf16[1024,1536]{0,1:T(8,128)(2,1)} async-done(((bf16[1024,192]{0,1:T(8,128)(2,1)}), bf16[1024,1536]{0,1:T(8,128)(2,1)}) %all-gather.40.cloned.1.call-update) | async-done | bytes 3145744 | tf_op jit(solution)/shard_map/all_gather | solution.py:89
  571.2 20.2 convolution_convert_fusion.2
  591.5 57.9 %reduce-scatter.14.cloned.1.call-done = bf16[2,256,1536]{2,1,0:T(8,128)(2,1)} async-done(((bf16[2,1024,1536]{2,1,0:T(8,128)(2,1)}), bf16[2,256,1536]{2,1,0:T(8,128)(2,1)}) %reduce-scatter.14.cloned.1.call-update) | async-done | bytes 1572880 | tf_op jit(solution)/shard_map/reduce_scatter | solution.py:201
  674.0 30.6 %all-gather.46.cloned.1.call-done = bf16[1536,768]{1,0:T(8,128)(2,1)} async-done(((bf16[192,768]{1,0:T(8,128)(2,1)}), bf16[1536,768]{1,0:T(8,128)(2,1)}) %all-gather.46.cloned.1.call-update) | async-done | bytes 2359312 | tf_op jit(solution)/shard_map/all_gather | solution.py:78
  711.4 46.3 %all-gather.50.cloned.1.call-done = bf16[1536,768]{1,0:T(8,128)(2,1)} async-done(((bf16[192,768]{1,0:T(8,128)(2,1)}), bf16[1536,768]{1,0:T(8,128)(2,1)}) %all-gather.50.cloned.1.call-update) | async-done | bytes 2359312 | tf_op jit(solution)/shard_map/all_gather | solution.py:77
  768.2 70.5 %all-gather.54.cloned.1.call-done = bf16[1536,1536]{1,0:T(8,128)(2,1)} async-done(((bf16[192,1536]{1,0:T(8,128)(2,1)}), bf16[1536,1536]{1,0:T(8,128)(2,1)}) %all-gather.54.cloned.1.call-update) | async-done | bytes 4718608 | tf_op jit(solution)/shard_map/all_gather | solution.py:76
  869.2 31.0 %all-gather.52.cloned.1.call-done = bf16[2,1024,768]{1,2,0:T(8,128)(2,1)} async-done(((bf16[2,256,768]{1,2,0:T(8,128)(2,1)}), bf16[2,1024,768]{1,2,0:T(8,128)(2,1)}) %all-gather.52.cloned.1.call-update) | async-done | bytes 3145744 | tf_op jit(solution)/shard_map/all_gather | solution.py:180
  901.6 57.2 %while.40 = (s32[]{:T(128)}, bf16[2,256,8,2,96]{1,4,3,2,0:T(8,128)(2,1)}, f32[2,8,2,256,1]{3,2,1,4,0:T(2,128)S(1)}, bf16[2,1024,768]{1,2,0:T(8,128)(2,1)}, s32[2...) while((s32[]{:T(128)}, ...), condition=%wide.region_12.13_spmd.clone, body=%wide.region_9.12_spmd.clone.sunk | while | flops 1662120192 | bytes 62538888 | solution.py:188
  991.6 50.5 %all-gather.62.cloned.1.call-done = bf16[1536,1024]{1,0:T(8,128)(2,1)} async-done(((bf16[192,1024]{1,0:T(8,128)(2,1)}), bf16[1536,1024]{1,0:T(8,128)(2,1)}) %all-gather.62.cloned.1.call-update) | async-done | bytes 3145744 | tf_op jit(solution)/shard_map/all_gather | solution.py:87
  1042.1 47.9 %all-gather.58.cloned.1.call-done = bf16[2,1024,1536]{2,1,0:T(8,128)(2,1)} async-done(((bf16[2,256,1536]{2,1,0:T(8,128)(2,1)}), bf16[2,1024,1536]{2,1,0:T(8,128)(2,1)}) %all-gather.58.cloned.1.call-update) | async-done | bytes 6291472 | tf_op jit(solution)/shard_map/all_gather | solution.py:193
  1101.7 49.8 %all-gather.60.cloned.1.call-done = bf16[1536,1024]{1,0:T(8,128)(2,1)} async-done(((bf16[192,1024]{1,0:T(8,128)(2,1)}), bf16[1536,1024]{1,0:T(8,128)(2,1)}) %all-gather.60.cloned.1.call-update) | async-done | bytes 3145744 | tf_op jit(solution)/shard_map/all_gather | solution.py:88
  1163.4 36.0 %all-gather.44.cloned.1.call-done = bf16[2,1024,1536]{2,1,0:T(8,128)(2,1)} async-done(((bf16[2,256,1536]{2,1,0:T(8,128)(2,1)}), bf16[2,1024,1536]{2,1,0:T(8,128)(2,1)}) %all-gather.44.cloned.1.call-update) | async-done | bytes 6291472 | tf_op jit(solution)/shard_map/all_gather | solution.py:253
  1199.4 61.6 %all-gather.42.cloned.1.call-done = bf16[1024,1536]{0,1:T(8,128)(2,1)} async-done(((bf16[1024,192]{0,1:T(8,128)(2,1)}), bf16[1024,1536]{0,1:T(8,128)(2,1)}) %all-gather.42.cloned.1.call-update) | async-done | bytes 3145744 | tf_op jit(solution)/shard_map/all_gather | solution.py:89
  1299.7 98.6 %reduce-scatter.16.cloned.1.call-done = f32[2,256,1536]{2,1,0:T(8,128)} async-done(((f32[2,1024,1536]{2,1,0:T(8,128)}), f32[2,256,1536]{2,1,0:T(8,128)}) %reduce-scatter.16.cloned.1.call-update) | async-done | bytes 3145744 | tf_op jit(solution)/shard_map/reduce_scatter | solution.py:265
  1417.0 172.9 %while.41 = (s32[]{:T(128)}, f32[2,256,8,2,96]{1,0,4,3,2:T(2,128)}, bf16[2,1024,768]{1,2,0:T(8,128)(2,1)}, bf16[2,1024,768]{2,1,0:T(8,128)(2,1)}, bf16[2,1024,76...) while((s32[]{:T(128)}, f32[2,256,8,2,96]{1,0,4,3,2:T(2,128)}, ...), condition=%wide.region_18.19_spmd.clone, body=%wide.region_16.18_spmd.clone.sunk | while | flops 4067029248 | bytes 192513344 | solution.py:329
  1467.2 32.3 %dynamic_update_slice.44 = f32[2,256,8,2,96]{1,0,4,3,2:T(2,128)} dynamic-update-slice(f32[2,256,8,2,96]{1,0,4,3,2:T(2,128)} %get-tuple-element.728, f32[1,256,8,2,96]{1,0,4,3,2:T(1,128)S(1)} %copy.145, s32[]{:T(128)S(6)} %copy.177, s32[]{:T(128)} %constant.103.clone.1..sunk, s32[]{:T(128)} %constant.103.clone.1..sunk, s32[]{:T(128)} %constant.103.clone.1..sunk, s32[]{:T(128)} %constant.103.clone.1..sunk) | dynamic-update-slice | bytes 3145732 | tf_op jit(solution)/shard_map/while/body/jit(dynamic_update_index_in_dim)/dynamic_update_slice | solution.py:329
  1553.5 32.3 %dynamic_update_slice.44 = f32[2,256,8,2,96]{1,0,4,3,2:T(2,128)} dynamic-update-slice(f32[2,256,8,2,96]{1,0,4,3,2:T(2,128)} %get-tuple-element.728, f32[1,256,8,2,96]{1,0,4,3,2:T(1,128)S(1)} %copy.145, s32[]{:T(128)S(6)} %copy.177, s32[]{:T(128)} %constant.103.clone.1..sunk, s32[]{:T(128)} %constant.103.clone.1..sunk, s32[]{:T(128)} %constant.103.clone.1..sunk, s32[]{:T(128)} %constant.103.clone.1..sunk) | dynamic-update-slice | bytes 3145732 | tf_op jit(solution)/shard_map/while/body/jit(dynamic_update_index_in_dim)/dynamic_update_slice | solution.py:329
  1673.2 72.7 %reduce-scatter.34.cloned.1.call-done = bf16[192,1024]{1,0:T(8,128)(2,1)} async-done(((bf16[1536,1024]{1,0:T(8,128)(2,1)}), bf16[192,1024]{1,0:T(8,128)(2,1)}) %reduce-scatter.34.cloned.1.call-update) | async-done | bytes 393232
  1748.4 74.8 %reduce-scatter.32.cloned.1.call-done = bf16[192,1024]{1,0:T(8,128)(2,1)} async-done(((bf16[1536,1024]{1,0:T(8,128)(2,1)}), bf16[192,1024]{1,0:T(8,128)(2,1)}) %reduce-scatter.32.cloned.1.call-update) | async-done | bytes 393232 | tf_op jit(solution)/shard_map/reduce_scatter | solution.py:277
  1825.2 75.5 %reduce-scatter.30.cloned.1.call-done = bf16[192,1024]{1,0:T(8,128)(2,1)} async-done(((bf16[1536,1024]{1,0:T(8,128)(2,1)}), bf16[192,1024]{1,0:T(8,128)(2,1)}) %reduce-scatter.30.cloned.1.call-update) | async-done | bytes 393232 | tf_op jit(solution)/shard_map/reduce_scatter | solution.py:274
  1913.9 86.0 %reduce-scatter.28.cloned.1.call-done = bf16[192,1536]{1,0:T(8,128)(2,1)} async-done(((bf16[1536,1536]{1,0:T(8,128)(2,1)}), bf16[192,1536]{1,0:T(8,128)(2,1)}) %reduce-scatter.28.cloned.1.call-update) | async-done | bytes 589840 | tf_op jit(solution)/shard_map/reduce_scatter | solution.py:53
  1999.9 99.1 %reduce-scatter.22.cloned.1.call-done = bf16[192,1536]{1,0:T(8,128)(2,1)} async-done(((bf16[1536,1536]{1,0:T(8,128)(2,1)}), bf16[192,1536]{1,0:T(8,128)(2,1)}) %reduce-scatter.22.cloned.1.call-update) | async-done | bytes 589840 | tf_op jit(solution)/shard_map/reduce_scatter | solution.py:44
  2099.0 71.8 %reduce-scatter.24.cloned.1.call-done = bf16[192,768]{1,0:T(8,128)(2,1)} async-done(((bf16[1536,768]{1,0:T(8,128)(2,1)}), bf16[192,768]{1,0:T(8,128)(2,1)}) %reduce-scatter.24.cloned.1.call-update) | async-done | bytes 294928 | tf_op jit(solution)/shard_map/reduce_scatter | solution.py:47
  2170.8 72.0 %reduce-scatter.26.cloned.1.call-done = bf16[192,768]{1,0:T(8,128)(2,1)} async-done(((bf16[1536,768]{1,0:T(8,128)(2,1)}), bf16[192,768]{1,0:T(8,128)(2,1)}) %reduce-scatter.26.cloned.1.call-update) | async-done | bytes 294928 | tf_op jit(solution)/shard_map/reduce_scatter | solution.py:50
  (385 shorter events, 679.7 us)
Async XLA Ops:
  7.9 108.5 %all-gather.22.cloned.1.call-start = ((), (), s32[]{:S(2)}) async-start(), calls=%async_computation.11 | async-start | bytes 2654208 | tf_op jit(solution)/shard_map/all_gather | solution.py:78
  8.7 188.6 %all-gather.30.cloned.1.call-start = ((), (), s32[]{:S(2)}) async-start(), calls=%async_computation.15 | async-start | bytes 5308416 | tf_op jit(solution)/shard_map/all_gather | solution.py:76
  9.4 218.4 %all-gather.28.cloned.1.call-start = ((), (), s32[]{:S(2)}) async-start(), calls=%async_computation.14 | async-start | bytes 3932160 | tf_op jit(solution)/shard_map/all_gather | solution.py:180
  72.8 185.9 %all-gather.24.cloned.1.call-start = ((), (), s32[]{:S(2)}) async-start(), calls=%async_computation.12 | async-start | bytes 3932160 | tf_op jit(solution)/shard_map/all_gather | solution.py:181
  120.7 218.6 %all-gather.32.cloned.1.call-start = ((), (), s32[]{:S(2)}) async-start(), calls=%async_computation.16 | async-start | bytes 5308416 | tf_op jit(solution)/shard_map/all_gather | solution.py:79
  121.3 279.0 %all-gather.36.cloned.1.call-start = ((), (), s32[]{:S(2)}) async-start(), calls=%async_computation.18 | async-start | bytes 3538944 | tf_op jit(solution)/shard_map/all_gather | solution.py:87
  122.0 326.7 %all-gather.34.cloned.1.call-start = ((), (), s32[]{:S(2)}) async-start(), calls=%async_computation.17 | async-start | bytes 7864320 | tf_op jit(solution)/shard_map/all_gather | solution.py:193
  347.3 162.8 %all-gather.38.cloned.1.call-start = ((), (), s32[]{:S(2)}) async-start(), calls=%async_computation.19 | async-start | bytes 3538944 | tf_op jit(solution)/shard_map/all_gather | solution.py:88
  348.0 223.2 %all-gather.40.cloned.1.call-start = ((), (), s32[]{:S(2)}) async-start(), calls=%async_computation.20 | async-start | bytes 3538944 | tf_op jit(solution)/shard_map/all_gather | solution.py:89
  348.6 300.8 %reduce-scatter.14.cloned.1.call-start = ((), (), s32[]{:S(2)}) async-start(), calls=%async_computation.21 | async-start | bytes 7864320 | tf_op jit(solution)/shard_map/reduce_scatter | solution.py:201
  591.5 113.2 %all-gather.46.cloned.1.call-start = ((), (), s32[]{:S(2)}) async-start(), calls=%async_computation.24 | async-start | bytes 2654208 | tf_op jit(solution)/shard_map/all_gather | solution.py:78
  653.4 104.4 %all-gather.50.cloned.1.call-start = ((), (), s32[]{:S(2)}) async-start(), calls=%async_computation.26 | async-start | bytes 2654208 | tf_op jit(solution)/shard_map/all_gather | solution.py:77
  654.1 184.5 %all-gather.54.cloned.1.call-start = ((), (), s32[]{:S(2)}) async-start(), calls=%async_computation.28 | async-start | bytes 5308416 | tf_op jit(solution)/shard_map/all_gather | solution.py:76
  654.7 214.5 %all-gather.48.cloned.1.call-start = ((), (), s32[]{:S(2)}) async-start(), calls=%async_computation.25 | async-start | bytes 3932160 | tf_op jit(solution)/shard_map/all_gather | solution.py:181
  710.9 189.4 %all-gather.52.cloned.1.call-start = ((), (), s32[]{:S(2)}) async-start(), calls=%async_computation.27 | async-start | bytes 3932160 | tf_op jit(solution)/shard_map/all_gather | solution.py:180
  766.7 214.3 %all-gather.56.cloned.1.call-start = ((), (), s32[]{:S(2)}) async-start(), calls=%async_computation.29 | async-start | bytes 5308416 | tf_op jit(solution)/shard_map/all_gather | solution.py:79
  767.3 274.8 %all-gather.62.cloned.1.call-start = ((), (), s32[]{:S(2)}) async-start(), calls=%async_computation.32 | async-start | bytes 3538944 | tf_op jit(solution)/shard_map/all_gather | solution.py:87
  768.0 322.1 %all-gather.58.cloned.1.call-start = ((), (), s32[]{:S(2)}) async-start(), calls=%async_computation.30 | async-start | bytes 7864320 | tf_op jit(solution)/shard_map/all_gather | solution.py:193
  989.5 162.0 %all-gather.60.cloned.1.call-start = ((), (), s32[]{:S(2)}) async-start(), calls=%async_computation.31 | async-start | bytes 3538944 | tf_op jit(solution)/shard_map/all_gather | solution.py:88
  990.1 209.4 %all-gather.44.cloned.1.call-start = ((), (), s32[]{:S(2)}) async-start(), calls=%async_computation.23 | async-start | bytes 7864320 | tf_op jit(solution)/shard_map/all_gather | solution.py:253
  990.8 270.3 %all-gather.42.cloned.1.call-start = ((), (), s32[]{:S(2)}) async-start(), calls=%async_computation.22 | async-start | bytes 3538944 | tf_op jit(solution)/shard_map/all_gather | solution.py:89
  991.6 406.8 %reduce-scatter.16.cloned.1.call-start = ((), (), s32[]{:S(2)}) async-start(), calls=%async_computation.33 | async-start | bytes 15728640 | tf_op jit(solution)/shard_map/reduce_scatter | solution.py:265
  1299.7 351.1 %reduce-scatter.18.cloned.1.call-start = ((), (), s32[]{:S(2)}) async-start(), calls=%async_computation.34 | async-start | bytes 3932160 | tf_op jit(solution)/shard_map/reduce_scatter | solution.py:333
  1589.9 78.6 %reduce-scatter.20.cloned.1.call-start = ((), (), s32[]{:S(2)}) async-start(), calls=%async_computation.35 | async-start | bytes 3932160 | tf_op jit(solution)/shard_map/reduce_scatter | solution.py:336
  1590.7 155.3 %reduce-scatter.34.cloned.1.call-start = ((), (), s32[]{:S(2)}) async-start(), calls=%async_computation.42 | async-start | bytes 3538944
  1609.3 213.9 %reduce-scatter.32.cloned.1.call-start = ((), (), s32[]{:S(2)}) async-start(), calls=%async_computation.41 | async-start | bytes 3538944 | tf_op jit(solution)/shard_map/reduce_scatter | solution.py:277
  1620.7 280.0 %reduce-scatter.30.cloned.1.call-start = ((), (), s32[]{:S(2)}) async-start(), calls=%async_computation.40 | async-start | bytes 3538944 | tf_op jit(solution)/shard_map/reduce_scatter | solution.py:274
  1632.1 367.7 %reduce-scatter.28.cloned.1.call-start = ((), (), s32[]{:S(2)}) async-start(), calls=%async_computation.39 | async-start | bytes 5308416 | tf_op jit(solution)/shard_map/reduce_scatter | solution.py:53
  1639.7 459.3 %reduce-scatter.22.cloned.1.call-start = ((), (), s32[]{:S(2)}) async-start(), calls=%async_computation.36 | async-start | bytes 5308416 | tf_op jit(solution)/shard_map/reduce_scatter | solution.py:44
  1650.7 520.1 %reduce-scatter.24.cloned.1.call-start = ((), (), s32[]{:S(2)}) async-start(), calls=%async_computation.37 | async-start | bytes 2654208 | tf_op jit(solution)/shard_map/reduce_scatter | solution.py:47
  1658.2 584.6 %reduce-scatter.26.cloned.1.call-start = ((), (), s32[]{:S(2)}) async-start(), calls=%async_computation.38 | async-start | bytes 2654208 | tf_op jit(solution)/shard_map/reduce_scatter | solution.py:50
  1672.5 619.5 %all-reduce.14.cloned.1.call-start = ((), (), s32[]{:S(2)}) async-start(), calls=%async_computation.43 | async-start | bytes 3538944 | tf_op jit(solution)/shard_map/psum | solution.py:64
  (59 other events, 2001.2 us)
Sparse Core Ops, SparseCore 0:
  10.2 53.2 all-gather.25
  65.6 50.7 all-gather.21
  118.6 78.6 all-gather.29
  199.3 28.4 all-gather.27
  229.8 28.9 all-gather.23
  260.8 78.4 all-gather.31
  341.5 58.7 all-gather.35
  402.4 46.2 all-gather.33
  450.9 59.1 all-gather.37
  512.1 59.0 all-gather.39
  591.6 57.8 reduce-scatter.13
  653.5 51.1 all-gather.45
  707.1 50.6 all-gather.49
  760.0 78.6 all-gather.53
  871.3 28.9 all-gather.51
  902.5 78.4 all-gather.55
  983.3 58.7 all-gather.61
  1043.7 46.2 all-gather.57
  1092.3 59.1 all-gather.59
  1153.1 46.2 all-gather.43
  1201.9 59.1 all-gather.41
  1299.8 98.5 reduce-scatter.15
  1590.0 37.9 reduce-scatter.17
  1630.6 37.9 reduce-scatter.19
  1672.4 73.5 reduce-scatter.33
  1749.8 73.3 reduce-scatter.31
  1827.2 73.3 reduce-scatter.29
  1904.7 95.0 reduce-scatter.27
  2003.8 95.1 reduce-scatter.21
  2102.9 67.8 reduce-scatter.23
  2174.7 68.0 reduce-scatter.25
  2245.4 46.5 all-reduce.13
  (1 shorter events, 28.4 us)
where the time goes:
time: 2320 us; the launch traced here: 2310 us
  waiting for transfers between devices  1630 us (70%)
  matrix products  333 us (14%)
  local copies, waits for them, and re-layouts  171 us (7%)
  other arithmetic  81.4 us (4%)
  blocking collectives  73 us (3%)
    all_gather x2, waiting for transfers between devices, gather_attention(): lax.all_gather(shard_query, 'fsdp', axis=0, tiled=True)  145 us
    all_gather x2, waiting for transfers between devices, gather_mlp(): lax.all_gather(shard_down, 'fsdp', axis=1, tiled=True)  123 us
    all_gather x2, waiting for transfers between devices, gather_mlp(): lax.all_gather(shard_gate, 'fsdp', axis=0, tiled=True)  102 us
    all_gather x2, waiting for transfers between devices, gather_mlp(): lax.all_gather(shard_up, 'fsdp', axis=0, tiled=True)  99.5 us
    reduce_scatter x1, waiting for transfers between devices, reduce_grads(): lax.psum_scatter(parts[0].astype(jnp.bfloat16), 'fsdp', scatter_dimension...  99.1 us
    reduce_scatter x1, waiting for transfers between devices, on_device(): lax.psum_scatter(part_normed_two.reshape(seq_count, length, model_width),...  98.6 us
    all_gather x2, waiting for transfers between devices, forward(): lax.all_gather(normed_two.reshape(seq_count, tok_local, model_width), 'co...  96.4 us
    reduce_scatter x1, waiting for transfers between devices, reduce_grads(): lax.psum_scatter(parts[3].astype(jnp.bfloat16), 'fsdp', scatter_dimension...  86 us
  transfers between devices with their start and end apart: 33, of which 32 were waited for; matrix products, arithmetic and copies ran while one was open for 14% of the time, Pallas kernels for 0%

commit v1 on v0

--- a/solution.py
+++ b/solution.py
@@ -1,8 +1,12 @@
+import functools
 import math
 
 import jax
 import jax.numpy as jnp
+import numpy as np
 from jax import lax
+from jax.experimental import pallas as pl
+from jax.experimental.pallas import tpu as pltpu
 from jax.sharding import PartitionSpec as P
 
 H = 16
@@ -90,7 +94,7 @@
     )
 
 
-def on_device(
+def on_device_general(
     tokens,
     segments,
     w_query,
@@ -227,12 +231,6 @@
     mlp_weights = gather_mlp(w_gate, w_up, w_down)
     state = forward(attn_weights, mlp_weights)
     output = state[0].astype(jnp.bfloat16).reshape(seq_count, tok_local, model_width)
-    fresh = lax.optimization_barrier(
-        (w_query, w_key, w_value, w_out, gain_attn, gain_mlp, w_gate, w_up, w_down, output)
-    )
-    attn_weights = gather_attention(fresh[0], fresh[1], fresh[2], fresh[3], fresh[4], fresh[5])
-    mlp_weights = gather_mlp(fresh[6], fresh[7], fresh[8])
-    state = forward(attn_weights, mlp_weights)
     (
         final,
         normed,
@@ -377,9 +375,1049 @@
     )
 
 
+BF = jnp.bfloat16
+F32 = jnp.float32
+LANES = 128
+HALF = HD // 2
+NEG = -1e30
+SCALE = 1.0 / math.sqrt(HD)
+SCALE_LOG2 = SCALE * math.log2(math.e)
+CTX = 4
+QH = H // CTX
+KH = KVH // CTX
+BLK = 256
+NT = (((1,), (1,)), ((), ()))
+TN = (((0,), (0,)), ((), ()))
+
+
+def dot_nt(a, b):
+    return lax.dot_general(a, b, NT, preferred_element_type=F32)
+
+
+def dot_tn(a, b):
+    return lax.dot_general(a, b, TN, preferred_element_type=F32)
+
+
+def dot_nn(a, b):
+    return jnp.dot(a, b, preferred_element_type=F32)
+
+
+def lane_iota(rows, width):
+    return lax.broadcasted_iota(jnp.int32, (rows, width), 1)
+
+
+def params(mb, sem):
+    return pltpu.CompilerParams(vmem_limit_bytes=mb << 20, dimension_semantics=sem)
+
+
+def cost(flops, nbytes, trans=0):
+    return pl.CostEstimate(flops=int(flops), bytes_accessed=int(nbytes), transcendentals=int(trans))
+
+
+def packed_columns():
+    src = []
+    for group in range(6):
+        if group < 4:
+            member, half = group // 2, group % 2
+            for g in range(KH):
+                head = 2 * g + member
+                src += [head * HD + half * HALF + t for t in range(HALF)]
+        else:
+            half = group - 4
+            for g in range(KH):
+                src += [QH * HD + g * HD + half * HALF + t for t in range(HALF)]
+        src += [(QH + KH) * HD + group * 32 + t for t in range(32)]
+    return np.array(src, np.int32)
+
+
+def pack_matrix():
+    n = (QH + 2 * KH) * HD
+    src = jnp.asarray(packed_columns())
+    return (lax.broadcasted_iota(jnp.int32, (n, n), 0) == src[None, :]).astype(BF)
+
+
+def rms_rows(x, gain):
+    r = lax.rsqrt(jnp.mean(x * x, axis=-1, keepdims=True) + EPSILON)
+    return x * r * gain
+
+
+def qkv_kernel(c_ref, f_ref, x0, x1, x2, x3, gain, w, cos, sin, normed, q, k, v, w_out, xs, ws):
+    @pl.when((pl.program_id(0) == 0) & (pl.program_id(1) == 0))
+    def _():
+        count, rows, _ = w.shape
+        for b in range(count):
+            ws[b * rows : (b + 1) * rows, :] = w[b ^ f_ref[0], :, 0 : ws.shape[1]]
+        w_out[...] = ws[...]
+
+    for d, ref in enumerate((x0, x1, x2, x3)):
+
+        @pl.when(pl.program_id(0) == d)
+        def _():
+            xs[...] = ref[0]
+
+    n = rms_rows(xs[...].astype(F32), gain[...]).astype(BF)
+    normed[...] = n
+    t = dot_nn(n, ws[...])
+    y = [t[:, LANES * p : LANES * (p + 1)] for p in range(6)]
+    c, s = cos[...], sin[...]
+    rot = []
+    for p in range(0, 6, 2):
+        rot += [y[p] * c - y[p + 1] * s, y[p + 1] * c + y[p] * s]
+    for p in range(4):
+        q[:, LANES * p : LANES * (p + 1)] = rot[p].astype(BF)
+    for p in range(2):
+        k[:, LANES * p : LANES * (p + 1)] = rot[4 + p].astype(BF)
+    quarter = lane_iota(y[0].shape[0], LANES) // 32
+
+    def place(parts):
+        out = jnp.ones_like(y[0])
+        for dst, p in parts:
+            piece = y[p] if dst == 3 else pltpu.roll(y[p], 32 * (dst + 1), 1)
+            out = jnp.where(quarter == dst, piece, out)
+        return out.astype(BF)
+
+    v[:, 0:128] = place(((0, 0), (1, 1), (2, 2), (3, 0)))
+    v[:, 128:256] = place(((0, 1), (1, 2)))
+    v[:, 256:384] = place(((2, 3), (3, 4)))
+    v[:, 384:512] = place(((0, 5), (1, 3), (2, 4), (3, 5)))
+
+
+def qkv_call(c, f, xs, gain, w, cos, sin):
+    seqs, tok, width = xs[0].shape
+    total = seqs * CTX * tok
+    cols = 768
+
+    def own(d):
+        return pl.BlockSpec(
+            (1, tok, width),
+            lambda i, s, c, f: (jnp.where(i == d, s, jnp.where(i < d, 0, seqs - 1)), 0, 0),
+        )
+
+    def rows(n):
+        return pl.BlockSpec((tok, n), lambda i, s, c, f: (s * CTX + (i ^ c[0]), 0))
+
+    return pl.pallas_call(
+        qkv_kernel,
+        grid_spec=pltpu.PrefetchScalarGridSpec(
+            num_scalar_prefetch=2,
+            grid=(CTX, seqs),
+            in_specs=[
+                own(0),
+                own(1),
+                own(2),
+                own(3),
+                pl.BlockSpec((1, width), lambda i, s, c, f: (0, 0)),
+                pl.BlockSpec(w.shape, lambda i, s, c, f: (0, 0, 0)),
+                rows(LANES),
+                rows(LANES),
+            ],
+            out_specs=[
+                rows(width),
+                rows(512),
+                rows(256),
+                rows(512),
+                pl.BlockSpec((width, cols), lambda i, s, c, f: (0, 0)),
+            ],
+            scratch_shapes=[pltpu.VMEM((tok, width), BF), pltpu.VMEM((width, cols), BF)],
+        ),
+        out_shape=[
+            jax.ShapeDtypeStruct((total, width), BF),
+            jax.ShapeDtypeStruct((total, 512), BF),
+            jax.ShapeDtypeStruct((total, 256), BF),
+            jax.ShapeDtypeStruct((total, 512), BF),
+            jax.ShapeDtypeStruct((width, cols), BF),
+        ],
+        compiler_params=params(48, ("arbitrary", "arbitrary")),
+        cost_estimate=cost(2 * total * width * 768, total * width * 4 + width * 768 * 4 + total * 3584),
+        name="qkv",
+    )(c, f, *xs, gain, w, cos, sin)
+
+
+def head_masks(rows):
+    lane = lane_iota(rows, 256)
+    inner_lane = lane % LANES
+    by_kv = [inner_lane < HALF, (inner_lane >= HALF) & (inner_lane < HD)]
+    in_mixed = [
+        lane < HD,
+        (lane >= HD) & (lane < 2 * HD),
+        (lane >= 64) & (lane < 64 + HD),
+        lane >= 64 + HD,
+    ]
+    return lane, by_kv, in_mixed
+
+
+def attend_kernel(js_ref, c_ref, q, k, v, start, mixed, lse, vt_s, m_s, o_s):
+    s_id, i = pl.program_id(0), pl.program_id(1)
+    blocks = k.shape[0] // BLK
+    lane, by_kv, in_mixed = head_masks(BLK)
+    sub = lax.broadcasted_iota(jnp.int32, (256, BLK), 0)
+    take_a = (sub < HD) | ((sub >= 192) & (sub < 224))
+    take_b = ((sub >= 64) & (sub < 64 + HD)) | (sub < 32)
+    zero = jnp.zeros((BLK, 256), BF)
+
+    @pl.when(i == 0)
+    def _():
+        for b in range(blocks):
+            vt_s[b] = jnp.transpose(v[b * BLK : (b + 1) * BLK, :])
+
+    m_s[...] = jnp.full_like(m_s, -jnp.inf)
+    o_s[...] = jnp.zeros_like(o_s)
+    col = i * BLK + lax.broadcasted_iota(jnp.int32, (BLK, BLK), 1)
+    first = start[0, 0]
+    low = js_ref[s_id * CTX + i]
+
+    def step(t, _):
+        j = i - t
+        kb = k[pl.ds(pl.multiple_of(j * BLK, BLK), BLK), :]
+        row = j * BLK + lax.broadcasted_iota(jnp.int32, (BLK, BLK), 0)
+        bias = jnp.where((row >= first) & (row <= col), 0.0, NEG)
+        for win, take in enumerate((take_a, take_b)):
+            vt = vt_s[j, 256 * win : 256 * (win + 1), :]
+            outs, alphas = [], []
+            for m in range(2):
+                h = 2 * win + m
+                qh = jnp.where(by_kv[win], q[:, 256 * m : 256 * (m + 1)], zero)
+                sc = dot_nt(kb, qh) * SCALE_LOG2 + bias
+                m_old = m_s[h : h + 1, :]
+                m_new = jnp.maximum(m_old, jnp.max(sc, axis=0, keepdims=True))
+                p = jnp.exp2(sc - m_new)
+                alphas.append(jnp.exp2(m_old - m_new))
+                m_s[h : h + 1, :] = m_new
+                outs.append(dot_nn(vt, p.astype(BF)))
+            o_s[win] = o_s[win] * jnp.where(take, alphas[0], alphas[1]) + jnp.where(take, outs[0], outs[1])
+        return 0
+
+    lax.fori_loop(0, i - low + 1, step, 0)
+    sums = [o_s[0, 192:193, :], o_s[0, 224:225, :], o_s[1, 0:1, :], o_s[1, 32:33, :]]
+    inv = [1.0 / x for x in sums]
+    a = jnp.transpose(o_s[0] * jnp.where(take_a, inv[0], inv[1]))
+    b = jnp.transpose(o_s[1] * jnp.where(take_b, inv[2], inv[3]))
+    mixed[0, 0, :, 0:128] = a[:, 0:128].astype(BF)
+    mixed[0, 0, :, 128:256] = jnp.where(lane[:, :LANES] < 64, a[:, 128:256], b[:, 0:128]).astype(BF)
+    mixed[0, 0, :, 256:384] = b[:, 128:256].astype(BF)
+    lse[0, 0] = jnp.zeros_like(lse[0, 0])
+    for h in range(QH):
+        lse[0, 0, h : h + 1, :] = m_s[h : h + 1, :] + jnp.log2(sums[h])
+
+
+def attend_call(c, js, q, k, v, start, seqs, length):
+    blocks = length // BLK
+    return pl.pallas_call(
+        attend_kernel,
+        grid_spec=pltpu.PrefetchScalarGridSpec(
+            num_scalar_prefetch=2,
+            grid=(seqs, blocks),
+            in_specs=[
+                pl.BlockSpec((BLK, 512), lambda s, i, js, c: (s * CTX + i, 0)),
+                pl.BlockSpec((length, 256), lambda s, i, js, c: (s, 0)),
+                pl.BlockSpec((length, 512), lambda s, i, js, c: (s, 0)),
+                pl.BlockSpec((1, 1, 1, BLK), lambda s, i, js, c: (s, i, 0, 0)),
+            ],
+            out_specs=[
+                pl.BlockSpec((1, 1, BLK, QH * HD), lambda s, i, js, c: (i ^ c[0], s, 0, 0)),
+                pl.BlockSpec((1, 1, 8, BLK), lambda s, i, js, c: (s, i, 0, 0)),
+            ],
+            scratch_shapes=[
+                pltpu.VMEM((blocks, 512, BLK), BF),
+                pltpu.VMEM((8, BLK), F32),
+                pltpu.VMEM((2, 256, BLK), F32),
+            ],
+        ),
+        out_shape=[
+            jax.ShapeDtypeStruct((CTX, seqs, BLK, QH * HD), BF),
+            jax.ShapeDtypeStruct((seqs, blocks, 8, BLK), F32),
+        ],
+        compiler_params=params(40, ("arbitrary", "arbitrary")),
+        cost_estimate=cost(6e9, 8e6, 4e6),
+        name="attend",
+    )(js, c, q, k, v, start)
+
+
+def attend_back_kernel(
+    js_ref, c_ref, q, k, v, o, d0, d1, d23, lse, start, cos, sin, out, do_s, dl_s, kt_s, dq_s, dk_s, dv_s
+):
+    s_id = pl.program_id(0)
+    c = c_ref[0]
+    blocks = q.shape[0] // BLK
+    lane, by_kv, in_mixed = head_masks(BLK)
+    zero = jnp.zeros((BLK, 256), BF)
+    mixed_lane = lane_iota(8, QH * HD)
+    mixed_row = lax.broadcasted_iota(jnp.int32, (8, QH * HD), 0)
+    picks = (mixed_lane // HD == mixed_row).astype(F32)
+    for d in range(CTX):
+        b = d ^ c
+        rows = pl.ds(pl.multiple_of(b * BLK, BLK), BLK)
+        g = d0[0, 0] if d == 0 else d1[0] if d == 1 else d23[d - 2, 0]
+        do_s[rows, :] = g
+        prod = g.astype(F32) * o[d, 0].astype(F32)
+        dl_s[b] = lax.dot_general(
+            picks, prod, NT, preferred_element_type=F32, precision=lax.Precision.HIGHEST
+        )
+    for b in range(blocks):
+        kt_s[b] = jnp.transpose(k[b * BLK : (b + 1) * BLK, :])
+    sub_in = lax.broadcasted_iota(jnp.int32, (256, BLK), 0) % LANES
+    sub_kv = [sub_in < HALF, (sub_in >= HALF) & (sub_in < HD)]
+    dq_s[...] = jnp.zeros_like(dq_s)
+    dk_s[...] = jnp.zeros_like(dk_s)
+    dv_s[...] = jnp.zeros_like(dv_s)
+
+    def outer(i, _):
+        qs = pl.ds(pl.multiple_of(i * BLK, BLK), BLK)
+        col = i * BLK + lax.broadcasted_iota(jnp.int32, (BLK, BLK), 1)
+        first = start[0, i]
+        delta = dl_s[i]
+        logs = lse[0, i]
+
+        def step(t, _):
+            j = i - t
+            ks = pl.ds(pl.multiple_of(j * BLK, BLK), BLK)
+            kb = k[ks, :]
+            kt = kt_s[j]
+            row = j * BLK + lax.broadcasted_iota(jnp.int32, (BLK, BLK), 0)
+            bias = jnp.where((row >= first) & (row <= col), 0.0, NEG)
+            dk = jnp.zeros((BLK, 256), F32)
+            dq = [jnp.zeros((256, BLK), F32) for _ in range(2)]
+            for win in range(KH):
+                vb = v[ks, 256 * win : 256 * (win + 1)]
+                kg = jnp.where(sub_kv[win], kt, zero)
+                dv = jnp.zeros((BLK, 256), F32)
+                for m in range(2):
+                    h = 2 * win + m
+                    qh = jnp.where(by_kv[win], q[qs, 256 * m : 256 * (m + 1)], zero)
+                    do = jnp.where(in_mixed[h], do_s[qs, LANES * win : LANES * win + 256], zero)
+                    sc = dot_nt(kb, qh) * SCALE_LOG2 + bias
+                    p = jnp.exp2(sc - logs[h : h + 1, :])
+                    dp = dot_nt(vb, do)
+                    ds = (p * (dp - delta[h : h + 1, :])).astype(BF)
+                    dv = dv + dot_nn(p.astype(BF), do)
+                    dk = dk + dot_nn(ds, qh)
+                    dq[m] = dq[m] + dot_nn(kg, ds)
+                dv_s[ks, 256 * win : 256 * (win + 1)] += dv
+            dk_s[ks, :] += dk
+            for m in range(2):
+                dq_s[i, m] += dq[m]
+            return 0
+
+        lax.fori_loop(0, i - js_ref[s_id * CTX + i] + 1, step, 0)
+        return 0
+
+    lax.fori_loop(0, blocks, outer, 0)
+    head_lane = lane[:, :LANES] < HD
+
+    def finish(i, _):
+        rows = pl.ds(pl.multiple_of(i * BLK, BLK), BLK)
+        cs, sn = cos[rows, :] * SCALE, sin[rows, :] * SCALE
+        a0, a1 = dv_s[rows, 0:128], dv_s[rows, 128:256]
+        b0, b1 = dv_s[rows, 256:384], dv_s[rows, 384:512]
+
+        def r(x, n):
+            return pltpu.roll(x, n, 1)
+
+        pieces = [
+            r(a0, 96) + a0,
+            r(a0, 64) + r(a1, 96),
+            r(a0, 32) + r(a1, 64),
+            r(b0, 32) + r(b1, 64),
+            b0 + r(b1, 32),
+            r(b1, 96) + b1,
+        ]
+        grads = []
+        for m in range(2):
+            dq = jnp.transpose(dq_s[i, m])
+            grads += [dq[:, 0:128], dq[:, 128:256]]
+        grads += [dk_s[rows, 0:128], dk_s[rows, 128:256]]
+        for p in range(0, 6, 2):
+            first_half = grads[p] * cs + grads[p + 1] * sn
+            second_half = grads[p + 1] * cs - grads[p] * sn
+            out[rows, LANES * p : LANES * (p + 1)] = jnp.where(head_lane, first_half, pieces[p]).astype(BF)
+            out[rows, LANES * (p + 1) : LANES * (p + 2)] = jnp.where(
+                head_lane, second_half, pieces[p + 1]
+            ).astype(BF)
+        return 0
+
+    lax.fori_loop(0, blocks, finish, 0)
+
+
+def attend_back_call(c, js, q, k, v, o, d0, d1, d23, lse, start, cos, sin, seqs, length):
+    blocks = length // BLK
+    width = QH * HD
+    return pl.pallas_call(
+        attend_back_kernel,
+        grid_spec=pltpu.PrefetchScalarGridSpec(
+            num_scalar_prefetch=2,
+            grid=(seqs,),
+            in_specs=[
+                pl.BlockSpec((length, 512), lambda s, js, c: (s, 0)),
+                pl.BlockSpec((length, 256), lambda s, js, c: (s, 0)),
+                pl.BlockSpec((length, 512), lambda s, js, c: (s, 0)),
+                pl.BlockSpec((CTX, 1, BLK, width), lambda s, js, c: (0, s, 0, 0)),
+                pl.BlockSpec((1, 1, BLK, width), lambda s, js, c: (0, s, 0, 0)),
+                pl.BlockSpec((1, BLK, width), lambda s, js, c: (s, 0, 0)),
+                pl.BlockSpec((2, 1, BLK, width), lambda s, js, c: (0, s, 0, 0)),
+                pl.BlockSpec((1, blocks, 8, BLK), lambda s, js, c: (s, 0, 0, 0)),
+                pl.BlockSpec((1, blocks, 1, BLK), lambda s, js, c: (s, 0, 0, 0)),
+                pl.BlockSpec((length, LANES), lambda s, js, c: (s, 0)),
+                pl.BlockSpec((length, LANES), lambda s, js, c: (s, 0)),
+            ],
+            out_specs=pl.BlockSpec((length, 768), lambda s, js, c: (s, 0)),
+            scratch_shapes=[
+                pltpu.VMEM((length, width), BF),
+                pltpu.VMEM((blocks, 8, BLK), F32),
+                pltpu.VMEM((blocks, 256, BLK), BF),
+                pltpu.VMEM((blocks, 2, 256, BLK), F32),
+                pltpu.VMEM((length, 256), F32),
+                pltpu.VMEM((length, 512), F32),
+            ],
+        ),
+        out_shape=jax.ShapeDtypeStruct((seqs * length, 768), BF),
+        compiler_params=params(48, ("arbitrary",)),
+        cost_estimate=cost(2e10, 1.2e7, 4e6),
+        name="attend_back",
+    )(js, c, q, k, v, o, d0, d1, d23, lse, start, cos, sin)
+
+
+def assemble_kernel(c_ref, f_ref, p0, p1, p2, p3, out):
+    quarter = p0.shape[-1]
+    for b in range(CTX):
+        for d, ref in enumerate((p0, p1, p2, p3)):
+
+            @pl.when((b ^ c_ref[0]) == d)
+            def _():
+                out[:, b * quarter : (b + 1) * quarter] = ref[0]
+
+
+def assemble_call(c, f, parts):
+    count, rows, quarter = parts[0].shape
+    part = pl.BlockSpec((1, rows, quarter), lambda b, c, f: (b ^ f[0], 0, 0))
+    return pl.pallas_call(
+        assemble_kernel,
+        grid_spec=pltpu.PrefetchScalarGridSpec(
+            num_scalar_prefetch=2,
+            grid=(count,),
+            in_specs=[part] * CTX,
+            out_specs=pl.BlockSpec((rows, CTX * quarter), lambda b, c, f: (b, 0)),
+        ),
+        out_shape=jax.ShapeDtypeStruct((count * rows, CTX * quarter), BF),
+        compiler_params=params(20, ("arbitrary",)),
+        cost_estimate=cost(0, count * rows * quarter * 16),
+        name="assemble",
+    )(c, f, *parts)
+
+
+def out_kernel(c_ref, x, m0, m1, m2, m3, w, gain, resid, normed):
+    c = c_ref[0]
+    acc = x[0].astype(F32)
+    for d, ref in enumerate((m0, m1, m2, m3)):
+        rows = pl.ds(pl.multiple_of((d ^ c) * (QH * HD), QH * HD), QH * HD)
+        acc = acc + dot_nn(ref[0, 0], w[rows, :])
+    resid[0] = acc
+    normed[0] = rms_rows(acc, gain[...]).astype(BF)
+
+
+def out_call(c, x, mixed, r1, r2, w, gain):
+    seqs, tok, width = x.shape
+    inner_w = QH * HD
+
+    def slot(n):
+        return pl.BlockSpec((1, 1, tok, inner_w), lambda s, c: (n, s, 0, 0))
+
+    tile = pl.BlockSpec((1, tok, width), lambda s, c: (s, 0, 0))
+    return pl.pallas_call(
+        out_kernel,
+        grid_spec=pltpu.PrefetchScalarGridSpec(
+            num_scalar_prefetch=1,
+            grid=(seqs,),
+            in_specs=[
+                tile,
+                slot(0),
+                slot(0),
+                slot(0),
+                slot(1),
+                pl.BlockSpec((H * HD, width), lambda s, c: (0, 0)),
+                pl.BlockSpec((1, width), lambda s, c: (0, 0)),
+            ],
+            out_specs=[tile, tile],
+        ),
+        out_shape=[
+            jax.ShapeDtypeStruct((seqs, tok, width), F32),
+            jax.ShapeDtypeStruct((seqs, tok, width), BF),
+        ],
+        compiler_params=params(48, ("arbitrary",)),
+        cost_estimate=cost(2 * seqs * tok * width * width, width * width * 2 + seqs * tok * width * 10),
+        name="out_proj",
+    )(c, x, mixed, r1, r2, r2, w, gain)
+
+
+def rms_back(v, gain, dy):
+    r = lax.rsqrt(jnp.mean(v * v, axis=-1, keepdims=True) + EPSILON)
+    dyg = dy * gain
+    inner_sum = jnp.mean(dyg * v, axis=-1, keepdims=True)
+    return r * dyg - v * (r * r * r * inner_sum), dy * v * r
+
+
+def out_back_kernel(c_ref, part_a, part_b, resid, gain, dy, w, dresid, dattn, dmixed, dgain):
+    c = c_ref[0]
+    dn = part_a[0].astype(F32) + part_b[0].astype(F32)
+    dr, dg = rms_back(resid[0], gain[...], dn)
+    total = dy[0].astype(F32) + dr
+    dresid[0] = total
+    low = total.astype(BF)
+    dattn[0] = low
+    dgain[0] = jnp.broadcast_to(jnp.sum(dg, axis=0, keepdims=True), dgain.shape[1:])
+    for d in range(CTX):
+        rows = pl.ds(pl.multiple_of((d ^ c) * (QH * HD), QH * HD), QH * HD)
+        dmixed[d, 0] = dot_nt(low, w[rows, :]).astype(BF)
+
+
+def out_back_call(c, part_a, part_b, resid, gain, dy, w):
+    seqs, tok, width = dy.shape
+    inner_w = QH * HD
+    tile = pl.BlockSpec((1, tok, width), lambda s, c: (s, 0, 0))
+    return pl.pallas_call(
+        out_back_kernel,
+        grid_spec=pltpu.PrefetchScalarGridSpec(
+            num_scalar_prefetch=1,
+            grid=(seqs,),
+            in_specs=[
+                tile,
+                tile,
+                tile,
+                pl.BlockSpec((1, width), lambda s, c: (0, 0)),
+                tile,
+                pl.BlockSpec((H * HD, width), lambda s, c: (0, 0)),
+            ],
+            out_specs=[
+                tile,
+                tile,
+                pl.BlockSpec((CTX, 1, tok, inner_w), lambda s, c: (0, s, 0, 0)),
+                pl.BlockSpec((1, 8, width), lambda s, c: (s, 0, 0)),
+            ],
+        ),
+        out_shape=[
+            jax.ShapeDtypeStruct((seqs, tok, width), F32),
+            jax.ShapeDtypeStruct((seqs, tok, width), BF),
+            jax.ShapeDtypeStruct((CTX, seqs, tok, inner_w), BF),
+            jax.ShapeDtypeStruct((seqs, 8, width), F32),
+        ],
+        compiler_params=params(56, ("arbitrary",)),
+        cost_estimate=cost(2 * seqs * tok * width * width, width * width * 2 + seqs * tok * width * 20),
+        name="out_back",
+    )(c, part_a, part_b, resid, gain, dy, w)
+
+
+def mlp_kernel(n2, dy, wg, wu, wd, hidden, grads):
+    n, g_out = n2[...], dy[...]
+    gate = dot_nn(n, wg[...])
+    up = dot_nn(n, wu[...])
+    dh = dot_nn(g_out, wd[...])
+    sig = 1.0 / (1.0 + jnp.exp(-gate))
+    act = gate * sig
+    hidden[...] = (act * up).astype(BF)
+    cols = wg.shape[1]
+    grads[0] = (dh * up * (sig + act * (1.0 - sig))).astype(BF)
+    grads[1] = (dh * act).astype(BF)
+
+
+def mlp_call(n2, dy, w):
+    rows, width = n2.shape
+    ff = w.shape[1] // 3
+    tile = BLK
+    steps = ff // tile
+    full = pl.BlockSpec((rows, width), lambda j: (0, 0))
+    return pl.pallas_call(
+        mlp_kernel,
+        grid=(steps,),
+        in_specs=[
+            full,
+            full,
+            pl.BlockSpec((width, tile), lambda j: (0, j)),
+            pl.BlockSpec((width, tile), lambda j: (0, j + steps)),
+            pl.BlockSpec((width, tile), lambda j: (0, j + 2 * steps)),
+        ],
+        out_specs=[
+            pl.BlockSpec((rows, tile), lambda j: (0, j)),
+            pl.BlockSpec((2, rows, tile), lambda j: (0, 0, j)),
+        ],
+        out_shape=[
+            jax.ShapeDtypeStruct((rows, ff), BF),
+            jax.ShapeDtypeStruct((2, rows, ff), BF),
+        ],
+        compiler_params=params(40, ("arbitrary",)),
+        cost_estimate=cost(6 * rows * width * ff, width * ff * 6 + rows * width * 4 + rows * ff * 6, rows * ff),
+        name="mlp",
+    )(n2, dy, w, w, w)
+
+
+def sum_nt_kernel(slots, *refs):
+    count = len(slots)
+    out = refs[-1]
+    acc = None
+    for n in range(count):
+        left = refs[n]
+        part = dot_nt(left[0] if len(left.shape) == 3 else left[...], refs[count + n][...])
+        acc = part if acc is None else acc + part
+    out[...] = acc.astype(out.dtype)
+
+
+def sum_nt_call(terms, tile):
+    rows, k = terms[0][0].shape[-2:]
+    n = terms[0][2].shape[0]
+    lefts, rights = [], []
+    for array, slot, weight, window in terms:
+        if slot is None:
+            lefts.append(pl.BlockSpec((rows, k), lambda j: (0, 0)))
+        else:
+            lefts.append(pl.BlockSpec((1, rows, k), functools.partial(lambda slot, j: (slot, 0, 0), slot)))
+        rights.append(pl.BlockSpec((tile, k), functools.partial(lambda window, j: (j, window), window)))
+    count = len(terms)
+    return pl.pallas_call(
+        functools.partial(sum_nt_kernel, tuple(t[1] for t in terms)),
+        grid=(n // tile,),
+        in_specs=lefts + rights,
+        out_specs=pl.BlockSpec((rows, tile), lambda j: (0, j)),
+        out_shape=jax.ShapeDtypeStruct((rows, n), BF),
+        compiler_params=params(40, ("arbitrary",)),
+        cost_estimate=cost(2 * rows * k * n * count, 2 * count * (rows * k + n * k) + 2 * rows * n),
+        name="sum_nt",
+    )(*[t[0] for t in terms], *[t[2] for t in terms])
+
+
+def mlp_gram_kernel(count, *refs):
+    dys, n2s = refs[:count], refs[count : 2 * count]
+    hid, gu = refs[2 * count : 3 * count], refs[3 * count : 4 * count]
+    out = refs[-1]
+
+    @pl.when(pl.program_id(0) == 0)
+    def _():
+        acc = dot_tn(dys[0][...], hid[0][...])
+        for n in range(1, count):
+            acc = acc + dot_tn(dys[n][...], hid[n][...])
+        out[...] = acc.astype(out.dtype)
+
+    @pl.when(pl.program_id(0) != 0)
+    def _():
+        acc = dot_tn(n2s[0][...], gu[0][0])
+        for n in range(1, count):
+            acc = acc + dot_tn(n2s[n][...], gu[n][0])
+        out[...] = acc.astype(out.dtype)
+
+
+def mlp_gram_call(dys, n2s, hid, gu, tile_m):
+    rows, m = dys[0].shape
+    k = hid[0].shape[1]
+    count = len(dys)
+    return pl.pallas_call(
+        functools.partial(mlp_gram_kernel, count),
+        grid=(3, m // tile_m),
+        in_specs=[pl.BlockSpec((rows, tile_m), lambda j, i: (0, jnp.where(j == 0, i, m // tile_m - 1)))] * count
+        + [pl.BlockSpec((rows, tile_m), lambda j, i: (0, jnp.where(j == 0, 0, i)))] * count
+        + [pl.BlockSpec((rows, k), lambda j, i: (0, 0))] * count
+        + [pl.BlockSpec((1, rows, k), lambda j, i: (jnp.maximum(j - 1, 0), 0, 0))] * count,
+        out_specs=pl.BlockSpec((tile_m, k), lambda j, i: (i, j)),
+        out_shape=jax.ShapeDtypeStruct((m, 3 * k), BF),
+        compiler_params=params(56, ("arbitrary", "arbitrary")),
+        cost_estimate=cost(6 * rows * m * k * count, count * rows * (2 * m + 3 * k) * 2 + m * 3 * k * 2),
+        name="mlp_gram",
+    )(*dys, *n2s, *hid, *gu)
+
+
+def split_gram_kernel(f_ref, left, right, extra, mine, theirs):
+    acc = dot_tn(left[...], right[...]).astype(BF)
+    rows = mine.shape[1]
+    k = right.shape[1]
+    side = f_ref[0] % 2
+
+    @pl.when(side == 0)
+    def _():
+        mine[0, :, :k] = acc[:rows]
+        theirs[0, :, :k] = acc[rows:]
+        mine[0, :, k:] = extra[:rows]
+        theirs[0, :, k:] = extra[rows:]
+
+    @pl.when(side != 0)
+    def _():
+        mine[0, :, :k] = acc[rows:]
+        theirs[0, :, :k] = acc[:rows]
+        mine[0, :, k:] = extra[rows:]
+        theirs[0, :, k:] = extra[:rows]
+
+
+def split_gram_call(f, left, right, extra):
+    tokens, m = left.shape
+    k, e = right.shape[1], extra.shape[1]
+    pair = m // 4
+    out = pl.BlockSpec((1, pair // 2, k + e), lambda z, f: (z ^ (f[0] // 2), 0, 0))
+    shape = jax.ShapeDtypeStruct((4, pair // 2, k + e), BF)
+    return pl.pallas_call(
+        split_gram_kernel,
+        grid_spec=pltpu.PrefetchScalarGridSpec(
+            num_scalar_prefetch=1,
+            grid=(4,),
+            in_specs=[
+                pl.BlockSpec((tokens, pair), lambda z, f: (0, z)),
+                pl.BlockSpec((tokens, k), lambda z, f: (0, 0)),
+                pl.BlockSpec((pair, e), lambda z, f: (z, 0)),
+            ],
+            out_specs=[out, out],
+        ),
+        out_shape=[shape, shape],
+        compiler_params=params(40, ("arbitrary",)),
+        cost_estimate=cost(2 * tokens * m * k, tokens * (m + k) * 2 + m * k * 2),
+        name="split_gram",
+    )(f, left, right, extra)
+
+
+def out_gram_kernel(c_ref, f_ref, m0, m1, m2, m3, dattn, out):
+    side = f_ref[0] % 2
+    rows = out.shape[3]
+    for d, ref in enumerate((m0, m1, m2, m3)):
+
+        @pl.when(pl.program_id(0) == d)
+        def _():
+            tok = ref.shape[1] * ref.shape[2]
+            acc = dot_tn(ref[0].reshape(tok, ref.shape[3]), dattn[...]).astype(BF)
+
+            @pl.when(side == 0)
+            def _():
+                out[0, 0, 0] = acc[:rows]
+                out[0, 1, 0] = acc[rows:]
+
+            @pl.when(side != 0)
+            def _():
+                out[0, 0, 0] = acc[rows:]
+                out[0, 1, 0] = acc[:rows]
+
+
+def out_gram_call(c, f, mixed, r1, r2, dattn):
+    seqs, tok, inner_w = mixed.shape[1:]
+    rows, width = dattn.shape
+    quarter = width // CTX
+
+    def slot(n):
+        return pl.BlockSpec((1, seqs, tok, inner_w), lambda d, e, c, f: (n, 0, 0, 0))
+
+    return pl.pallas_call(
+        out_gram_kernel,
+        grid_spec=pltpu.PrefetchScalarGridSpec(
+            num_scalar_prefetch=2,
+            grid=(CTX, CTX),
+            in_specs=[
+                slot(0),
+                slot(0),
+                slot(0),
+                slot(1),
+                pl.BlockSpec((rows, quarter), lambda d, e, c, f: (0, e ^ c[0])),
+            ],
+            out_specs=pl.BlockSpec(
+                (1, 2, 1, inner_w // 2, quarter), lambda d, e, c, f: (e, 0, d ^ c[0] ^ (f[0] // 2), 0, 0)
+            ),
+        ),
+        out_shape=jax.ShapeDtypeStruct((CTX, 2, 4, inner_w // 2, quarter), BF),
+        compiler_params=params(40, ("arbitrary", "arbitrary")),
+        cost_estimate=cost(2 * rows * width * width, width * width * 2 + rows * width * 4),
+        name="out_gram",
+    )(c, f, mixed, r1, r2, r2, dattn)
+
+
+def unpack_kernel(c_ref, s0, s1, s2, s3, perm, o0, o1, o2, o3, gq, gk, gv, gg, go):
+    c = c_ref[0]
+    qw, kw = QH * HD, KH * HD
+    n = perm.shape[0]
+    for b in range(CTX):
+        for d, (ref, out) in enumerate(((s0, o0), (s1, o1), (s2, o2), (s3, o3))):
+
+            @pl.when((b ^ c) == d)
+            def _():
+                flat = dot_nt(ref[:, :n], perm[...])
+                gq[:, b * qw : (b + 1) * qw] = flat[:, :qw]
+                gk[:, b * kw : (b + 1) * kw] = flat[:, qw : qw + kw]
+                gv[:, b * kw : (b + 1) * kw] = flat[:, qw + kw :]
+                go[:, b * qw : (b + 1) * qw] = out[...].astype(F32)
+
+    gg[...] = (
+        s0[:, n:].astype(F32) + s1[:, n:].astype(F32) + s2[:, n:].astype(F32) + s3[:, n:].astype(F32)
+    )
+
+
+def unpack_call(c, parts, perm, outs):
+    rows = parts[0].shape[0]
+    extra = parts[0].shape[1] - perm.shape[0]
+    vm = pl.BlockSpec(memory_space=pltpu.VMEM)
+    return pl.pallas_call(
+        unpack_kernel,
+        in_specs=[pl.BlockSpec(memory_space=pltpu.SMEM)] + [vm] * 9,
+        out_specs=[vm] * 5,
+        out_shape=[
+            jax.ShapeDtypeStruct((rows, H * HD), F32),
+            jax.ShapeDtypeStruct((rows, KVH * HD), F32),
+            jax.ShapeDtypeStruct((rows, KVH * HD), F32),
+            jax.ShapeDtypeStruct((rows, extra), F32),
+            jax.ShapeDtypeStruct((rows, CTX * outs[0].shape[1]), F32),
+        ],
+        compiler_params=pltpu.CompilerParams(vmem_limit_bytes=40 << 20),
+        cost_estimate=cost(1e9, 1e7),
+        name="unpack",
+    )(c, *parts, perm, *outs)
+
+
+def qkv_back_kernel(c_ref, g, w, out):
+    out[0, 0] = dot_nt(g[...], w[...]).astype(BF)
+
+
+def qkv_back_call(c, grads, w, seqs, base):
+    width = w.shape[0]
+    return pl.pallas_call(
+        qkv_back_kernel,
+        grid_spec=pltpu.PrefetchScalarGridSpec(
+            num_scalar_prefetch=1,
+            grid=(2, seqs),
+            in_specs=[
+                pl.BlockSpec((BLK, 768), lambda d, s, c: (s * CTX + ((d + base) ^ c[0]), 0)),
+                pl.BlockSpec((width, 768), lambda d, s, c: (0, 0)),
+            ],
+            out_specs=pl.BlockSpec((1, 1, BLK, width), lambda d, s, c: (d, s, 0, 0)),
+        ),
+        out_shape=jax.ShapeDtypeStruct((2, seqs, BLK, width), BF),
+        compiler_params=params(40, ("arbitrary", "arbitrary")),
+        cost_estimate=cost(4 * seqs * BLK * 768 * width, width * 768 * 2 + 2 * seqs * BLK * (width + 768) * 2),
+        name="qkv_back",
+    )(c, grads, w)
+
+
+def final_kernel(part_a, part_b, x, gain, dresid, out, dgain):
+    dn = part_a[0].astype(F32) + part_b[0].astype(F32)
+    dx, dg = rms_back(x[0].astype(F32), gain[...], dn)
+    out[0] = dresid[0] + dx
+    dgain[0] = jnp.broadcast_to(jnp.sum(dg, axis=0, keepdims=True), dgain.shape[1:])
+
+
+def final_call(part_a, part_b, x, gain, dresid):
+    seqs, tok, width = x.shape
+    tile = pl.BlockSpec((1, tok, width), lambda s: (s, 0, 0))
+    return pl.pallas_call(
+        final_kernel,
+        grid=(seqs,),
+        in_specs=[tile, tile, tile, pl.BlockSpec((1, width), lambda s: (0, 0)), tile],
+        out_specs=[tile, pl.BlockSpec((1, 8, width), lambda s: (s, 0, 0))],
+        out_shape=[
+            jax.ShapeDtypeStruct((seqs, tok, width), F32),
+            jax.ShapeDtypeStruct((seqs, 8, width), F32),
+        ],
+        compiler_params=params(40, ("arbitrary",)),
+        cost_estimate=cost(20 * seqs * tok * width, 14 * seqs * tok * width),
+        name="final",
+    )(part_a, part_b, x, gain, dresid)
+
+
+CORE = [(i, i ^ 1) for i in range(CTX)]
+ROW = [(i, i ^ 2) for i in range(CTX)]
+
+
+def swap_core(x):
+    return lax.ppermute(x, "context", CORE)
+
+
+def swap_row(x):
+    return lax.ppermute(x, "context", ROW)
+
+
+def gather_blocks(x):
+    far = swap_row(x)
+    near = swap_core(x)
+    return [x, near, far, swap_core(far)]
+
+
+def after(x, *first):
+    return lax.optimization_barrier((x,) + first)[0]
+
+
+def swap_fsdp(x, bit):
+    size = lax.axis_size("fsdp")
+    return lax.ppermute(x, "fsdp", [(i, i ^ bit) for i in range(size)])
+
+
+def gather_fsdp(x):
+    near = swap_fsdp(x, 2)
+    side = swap_fsdp(x, 1)
+    far = swap_fsdp(jnp.stack([x, near]), 4)
+    near_side = swap_fsdp(near, 1)
+    far_side = swap_fsdp(far, 1)
+    return jnp.stack([x, side, near, near_side, far[0], far_side[0], far[1], far_side[1]])
+
+
+def reduce_fsdp(mine, theirs):
+    a = add_low(mine, swap_fsdp(theirs, 1))
+    b = add_low(a[0:2], swap_fsdp(a[2:4], 4))
+    return add_low(b[0], swap_fsdp(b[1], 2))
+
+
+def add_low(a, b):
+    return (a.astype(F32) + b.astype(F32)).astype(BF)
+
+
+def on_device(
+    tokens,
+    segments,
+    w_query,
+    w_key,
+    w_value,
+    w_out,
+    w_gate,
+    w_up,
+    w_down,
+    gain_attn,
+    gain_mlp,
+    cotangent,
+):
+    seqs, tok, width = tokens.shape
+    rows = seqs * tok
+    length = tok * CTX
+    qkv_w = (QH + 2 * KH) * HD
+    ctx = lax.axis_index("context")
+    core = ctx % 2
+    c = ctx.astype(jnp.int32).reshape(1)
+
+    segs = gather_blocks(segments)
+    xs = gather_blocks(after(tokens, *segs))
+    dys = gather_blocks(after(cotangent, *xs))
+
+    perm = pack_matrix()
+    shard = jnp.concatenate(
+        [
+            lax.dynamic_slice_in_dim(w_query, ctx * (QH * HD), QH * HD, 1),
+            lax.dynamic_slice_in_dim(w_key, ctx * (KH * HD), KH * HD, 1),
+            lax.dynamic_slice_in_dim(w_value, ctx * (KH * HD), KH * HD, 1),
+        ],
+        axis=1,
+    )
+    shard = jnp.dot(shard, perm, preferred_element_type=F32).astype(BF)
+    gains = jnp.pad(jnp.stack([gain_attn, gain_mlp], axis=1), ((0, 0), (0, LANES - 2)))
+    shard = jnp.concatenate([shard, gains], axis=1)
+    fsdp = lax.axis_index("fsdp").astype(jnp.int32).reshape(1)
+    w_qkv = gather_fsdp(shard)
+    down_t = jnp.transpose(w_down)
+    ff = w_gate.shape[1] // 2
+    w_parts = []
+    for n in range(2):
+        cols = slice(n * ff, (n + 1) * ff)
+        part = jnp.concatenate([w_gate[:, cols], w_up[:, cols], down_t[:, cols]], axis=1)
+        if n:
+            part = after(part, *segs)
+        w_parts.append(lax.all_gather(part, "fsdp", axis=0, tiled=True))
+    gain_cols = w_qkv[:, :, qkv_w : qkv_w + 2]
+    gain_cols = jnp.concatenate(
+        [lax.dynamic_index_in_dim(gain_cols, b ^ fsdp[0], 0, keepdims=False) for b in range(8)], axis=0
+    )
+    gain_rows = jnp.transpose(gain_cols).astype(F32)
+    gain_a, gain_m = gain_rows[0:1], gain_rows[1:2]
+    quarter = width // CTX
+    out_part = gather_fsdp(after(lax.dynamic_slice_in_dim(w_out, ctx * quarter, quarter, 1), w_qkv))
+    out_parts = gather_blocks(out_part)
+    w_out_full = assemble_call(c, fsdp, out_parts)
+
+    seg_blocks = jnp.stack(segs)
+    whole_seg = jnp.concatenate(
+        [lax.dynamic_index_in_dim(seg_blocks, b ^ ctx, 0, keepdims=False) for b in range(CTX)], axis=1
+    )
+    index = jnp.arange(length, dtype=jnp.int32)
+    starts = jnp.concatenate(
+        [jnp.ones((seqs, 1), dtype=bool), whole_seg[:, 1:] != whole_seg[:, :-1]], axis=1
+    )
+    first = lax.cummax(jnp.where(starts, index[None, :], 0), axis=1)
+    positions = (index[None, :] - first).astype(F32).reshape(seqs * length, 1)
+    freq = np.zeros((LANES,), np.float32)
+    base = (THETA ** -(np.arange(HALF, dtype=np.float64) * 2.0 / HD)).astype(np.float32)
+    for g in range(KH):
+        freq[g * HALF : (g + 1) * HALF] = base
+    angles = positions * jnp.asarray(freq)[None, :]
+    cos, sin = jnp.cos(angles), jnp.sin(angles)
+    low_block = (first[:, ::BLK] // BLK).reshape(seqs * CTX).astype(jnp.int32)
+    first_rows = first.reshape(seqs, CTX, 1, BLK)
+
+    normed, q, k, v, w_packed = qkv_call(c, fsdp, xs, gain_a, w_qkv, cos, sin)
+    mixed, lse = attend_call(c, low_block, q, k, v, first_rows, seqs, length)
+    r1 = swap_core(jnp.stack([mixed[1], mixed[3]]))
+    r2 = swap_row(jnp.stack([mixed[2], r1[1]]))
+    resid, normed_two = out_call(c, tokens, mixed, r1, r2, w_out_full, gain_m)
+
+    n2s = [n.reshape(rows, width) for n in gather_blocks(normed_two)]
+    dys = [d.reshape(rows, width) for d in dys]
+    hiddens, grads, shares = [], [], []
+    for w in w_parts:
+        pairs = [mlp_call(n2s[d], dys[d], w) for d in range(CTX)]
+        hiddens.append([p[0] for p in pairs])
+        grads.append([p[1] for p in pairs])
+        gram = mlp_gram_call(dys, n2s, hiddens[-1], grads[-1], 512)
+        shares.append(gram)
+
+    def back_rows(d):
+        terms = [(grads[n][d], slot, w_parts[n], slot) for n in range(2) for slot in range(2)]
+        return sum_nt_call(terms, 512)
+
+    def down_rows(d):
+        return sum_nt_call([(hiddens[n][d], None, w_parts[n], 2) for n in range(2)], 512)
+
+    dn3, dn2, dn1, dn0 = [back_rows(d) for d in (3, 2, 1, 0)]
+    dn2 = add_low(dn2, swap_core(dn3))
+    dn_b = swap_row(dn2)
+    dn_a = add_low(dn0, swap_core(dn1))
+    s_one = lax.psum_scatter(shares[0], "fsdp", scatter_dimension=0, tiled=True)
+    s_two = lax.psum_scatter(after(shares[1], s_one), "fsdp", scatter_dimension=0, tiled=True)
+    dn_b = after(dn_b, dn_a, *shares)
+    dresid, dattn, dmixed, dgain_m = out_back_call(
+        c, dn_a.reshape(tokens.shape), dn_b.reshape(tokens.shape), resid, gain_m, cotangent, w_out_full
+    )
+
+    b1 = swap_core(jnp.stack([dmixed[1], dmixed[3]]))
+    b2 = swap_row(jnp.stack([dmixed[2], b1[1]]))
+    g_out = out_gram_call(c, fsdp, mixed, r1, r2, dattn.reshape(rows, width))
+    got = swap_core(jnp.stack([g_out[1], g_out[3]]))
+    downs = [down_rows(d) for d in range(CTX)]
+    down2 = add_low(downs[2], swap_core(downs[3]))
+    down_b = swap_row(down2)
+    down_a = add_low(downs[0], swap_core(downs[1]))
+    got_row = swap_row(add_low(g_out[2], got[1]))
+    g_out = add_low(add_low(g_out[0], got[0]), got_row)
+    b2 = after(b2, down2, down_a, s_one)
+    dqkv = attend_back_call(
+        c, low_block, q, k, v, mixed, dmixed, b1[0], b2, lse, first_rows, cos, sin, seqs, length
+    )
+    s_out = reduce_fsdp(g_out[0], g_out[1])
+
+    far = qkv_back_call(c, dqkv, w_packed, seqs, 2)
+    dx2 = add_low(far[0], swap_core(far[1]))
+    dx_b = swap_row(dx2)
+    gain_m_col = jnp.pad(jnp.sum(dgain_m[:, 0], axis=0)[:, None], ((0, 0), (1, LANES - 2)))
+    near = qkv_back_call(c, after(dqkv, dx2), w_packed, seqs, 0)
+    dx_a = add_low(near[0], swap_core(near[1]))
+    output = (
+        resid + down_a.astype(F32).reshape(resid.shape) + down_b.astype(F32).reshape(resid.shape)
+    ).astype(BF)
+    grad_tokens, dgain_a = final_call(dx_a, after(dx_b, s_two), tokens, gain_a, dresid)
+    gain_grads = jnp.pad(jnp.sum(dgain_a[:, 0], axis=0)[:, None], ((0, 0), (0, LANES - 1))) + gain_m_col
+    s_qkv = reduce_fsdp(*split_gram_call(fsdp, normed, dqkv, gain_grads.astype(BF)))
+    g_query, g_key, g_value, g_gain, g_w_out = unpack_call(
+        c, gather_blocks(s_qkv), perm, gather_blocks(s_out)
+    )
+    return (
+        output,
+        grad_tokens,
+        g_query,
+        g_key,
+        g_value,
+        g_w_out,
+        jnp.concatenate([s[:, ff : 2 * ff] for s in (s_one, s_two)], axis=1).astype(F32),
+        jnp.concatenate([s[:, 2 * ff :] for s in (s_one, s_two)], axis=1).astype(F32),
+        jnp.transpose(jnp.concatenate([s[:, :ff] for s in (s_one, s_two)], axis=1)).astype(F32),
+        g_gain[:, 0],
+        g_gain[:, 1],
+    )
+
+
 def solution(mesh):
+    split_heads = mesh.shape["context"] == CTX
     return jax.shard_map(
-        on_device,
+        on_device if split_heads else on_device_general,
         mesh=mesh,
         in_specs=(
             P("fsdp", "context", None),

time: 2320 us -> 677 us (0.29)
  waiting for transfers between devices: 1630 us -> 288 us
  matrix products: 333 us -> 0.65 us
  Pallas kernels: 0 us -> 217 us
  local copies, waits for them, and re-layouts: 171 us -> 63.5 us
  blocking collectives: 73 us -> 0 us
  starting transfers between devices: 2.31 us -> 52.4 us
  other arithmetic: 81.4 us -> 35.9 us
    all_gather x21 -> x2, waiting for transfers between devices: 883 us -> 0.02 us  [on_device(): w_parts.append(lax.all_gather(part, 'fsdp', axis=0, tiled=True))]
    reduce_scatter x10 -> x2, waiting for transfers between devices: 646 us -> 0.01 us  [the longest x1 0.01 us: on_device(): s_one = lax.psum_scatter(shares[0], 'fsdp', scatter_dimension=0, tiled=True)]
    dot_general x42 -> x1, matrix products: 311 us -> 0.65 us  [on_device(): shard = jnp.dot(shard, perm, preferred_element_type=F32).astype(BF)]
    ppermute x0 -> x52, waiting for transfers between devices: none -> 288 us  [the longest x16 150 us: swap_fsdp(): return lax.ppermute(x, 'fsdp', [(i, i ^ bit) for i in range(size)])]
    pallas_call x0 -> x30, Pallas kernels: none -> 217 us  [the longest x2 37.5 us: mlp_gram_call(): pl.pallas_call(functools.partial(mlp_gram_kernel, count), grid=(3, m // t...]
    unnamed x34 -> x4, waiting for transfers between devices: 81.9 us -> 0.07 us
    dynamic_update_slice x10 -> x0, local copies, waits for them, and re-layouts: 76.1 us -> none  [on_device(): lax.map(attend_back, (qrot, all_keys, all_values, segments, whole_seg, lo...]
    unnamed x3 -> x0, blocking collectives: 53.5 us -> none
  transfers between devices with their start and end apart: 33 -> 56, of which waited for: 32 -> 21; matrix products, arithmetic and copies ran while one was open for 14% -> 8% of each run, Pallas kernels for 0% -> 32%
where the time goes in v1:
time: 677 us; the launch traced here: 673 us
  waiting for transfers between devices  288 us (43%)
  Pallas kernels  217 us (32%)
  local copies, waits for them, and re-layouts  63.5 us (9%)
  starting transfers between devices  52.4 us (8%)
  other arithmetic  35.9 us (5%)
  between operations  15.6 us (2%)
    ppermute x16, waiting for transfers between devices, swap_fsdp(): return lax.ppermute(x, 'fsdp', [(i, i ^ bit) for i in range(size)])  150 us
    ppermute x13, waiting for transfers between devices, swap_row(): return lax.ppermute(x, 'context', ROW)  133 us
    unnamed x210, local copies, waits for them, and re-layouts  46.9 us
    pallas_call x2, Pallas kernels, mlp_gram_call(): pl.pallas_call(functools.partial(mlp_gram_kernel, count), grid=(3, m // t...  37.5 us
    pallas_call x8, Pallas kernels, mlp_call(): pl.pallas_call(mlp_kernel, grid=(steps,), in_specs=[full, full, pl.BlockS...  34.3 us
    pallas_call x1, Pallas kernels, attend_back_call(): pl.pallas_call(attend_back_kernel, grid_spec=pltpu.PrefetchScalarGridSpec...  31.5 us
    pallas_call x8, Pallas kernels, sum_nt_call(): pl.pallas_call(functools.partial(sum_nt_kernel, tuple((t[1] for t in term...  31.1 us
    ppermute x23, starting transfers between devices, swap_core(): return lax.ppermute(x, 'context', CORE)  25.9 us
  transfers between devices with their start and end apart: 56, of which 21 were waited for; matrix products, arithmetic and copies ran while one was open for 8% of the time, Pallas kernels for 32%

profile of v1, /device:TPU:1, one launch (start us, length us, event | category | flops | bytes accessed | tf_op | source)
XLA Modules:
  0.0 673.5 jit_solution(46281023882246224)
XLA Ops:
  29.2 5.3 multiply_sine_fusion
  35.8 37.6 %collective-permute-done.9 = bf16[2,192,896]{2,1,0:T(8,128)(2,1)S(1)} collective-permute-done((bf16[2,192,896]{2,1,0:T(8,128)(2,1)S(1)}, bf16[2,192,896]{2,1,0:T(8,128)(2,1)S(1)}, u32[]{:S(2)}, u32[]{:S(2)}) %collective-permute-start.9) | collective-permute-done | bytes 688160 | tf_op jit(solution)/shard_map/ppermute | solution.py:1236
  75.0 7.3 %collective-permute-start.5 = (bf16[2,256,1536]{2,1,0:T(8,128)(2,1)}, bf16[2,256,1536]{2,1,0:T(8,128)(2,1)}, u32[]{:S(2)}, u32[]{:S(2)}) collective-permute-start(bf16[2,256,1536]{2,1,0:T(8,128)(2,1)} %collective-permute-done.4.x2), channel_id=1, source_target_pairs={{0,1},{1,0},{2,3},{3,2},{4,5},{5,4},{6,7},{7,6},{8,9},{9,8},{10,11... | collective-permute-start | bytes 4718600 | tf_op jit(solution)/shard_map/ppermute | solution.py:1217
  82.3 20.4 %collective-permute-done.10 = bf16[2,192,896]{2,1,0:T(8,128)(2,1)S(1)} collective-permute-done((bf16[2,192,896]{2,1,0:T(8,128)(2,1)S(1)}, bf16[2,192,896]{2,1,0:T(8,128)(2,1)S(1)}, u32[]{:S(2)}, u32[]{:S(2)}) %collective-permute-start.10) | collective-permute-done | bytes 688160 | tf_op jit(solution)/shard_map/ppermute | solution.py:1236
  117.9 21.1 %collective-permute-done.16 = bf16[2,192,384]{2,1,0:T(8,128)(2,1)S(1)} collective-permute-done((bf16[2,192,384]{2,1,0:T(8,128)(2,1)S(1)}, bf16[2,192,384]{2,1,0:T(8,128)(2,1)S(1)}, u32[]{:S(2)}, u32[]{:S(2)}) %collective-permute-start.16) | collective-permute-done | bytes 294944 | tf_op jit(solution)/shard_map/ppermute | solution.py:1236
  139.5 5.9 collective-permute-done.17
  147.4 15.4 %qkv.1 = (bf16[2048,1536]{1,0:T(8,128)(2,1)}, bf16[2048,512]{1,0:T(8,128)(2,1)}, bf16[2048,256]{1,0:T(8,128)(2,1)S(1)}, bf16[2048,512]{1,0:T(8,128)(2,1)}, bf16[1536,768]{1,0:T(8,128)(2,1)}) custom-call(s32[1]{0:T(128)} %bitcast.c_ref, s32[1]{0:T(128)} %bitcast.9.f_ref, bf16[2,256,1536]{2,1,0:T(8,128)(2,1)S(1)} %copy-done.23, ...), custom_call_target="tpu_custom_call" | custom-call | flops 4831838208 | bytes 24641536 | tf_op jit(solution)/shard_map/qkv/pallas_call | solution.py:499
  166.3 18.0 %attend.1 = (bf16[4,2,256,384]{3,2,1,0:T(8,128)(2,1)S(1)}, f32[2,4,8,256]{3,2,1,0:T(8,128)S(1)}) custom-call(s32[8]{0:T(128)S(1)} %reshape.150.js_ref, s32[1]{0:T(128)} %bitcast.c_ref, bf16[2048,512]{1,0:T(8,128)(2,1)S(1)} %copy-done.71, bf16[2048,256]{1,0:T(8,128)(2,1)S(1)} %get-tuple-element.60.k, bf16[2048,512]{1,0:T(8,128)(2,1)S(1)} %copy-done.72, ...), custom_call_target="tpu_custom_call" | custom-call | flops 6000000000 | bytes 8000000 | tf_op jit(solution)/shard_map/attend/pallas_call | solution.py:605
  197.0 12.1 %collective-permute-done.12.m2.m3 = bf16[2,2,256,384]{3,2,1,0:T(8,128)(2,1)S(1)} collective-permute-done((bf16[2,2,256,384]{3,2,1,0:T(8,128)(2,1)S(1)}, bf16[2,2,256,384]{3,2,1,0:T(8,128)(2,1)S(1)}, u32[]{:S(2)}, u32[]{:S(2)}) %collective-permute-start.12) | collective-permute-done | bytes 786464 | tf_op jit(solution)/shard_map/ppermute | solution.py:1221
  209.1 7.6 %out_proj.1 = (f32[2,256,1536]{2,1,0:T(8,128)}, bf16[2,256,1536]{2,1,0:T(8,128)(2,1)S(1)}) custom-call(s32[1]{0:T(128)} %bitcast.c_ref, bf16[2,256,1536]{2,1,0:T(8,128)(2,1)S(1)} %copy-done.24, bf16[4,2,256,384]{3,2,1,0:T(8,128)(2,1)} %copy-done.12, bf16[2,2,256,384]{3,2,1,0:T(8,128)(2,1)S(1)} %collective-permute-done.11.m1, ...), custom_call_target="tpu_custom_call" | custom-call | flops 2415919104 | bytes 12582912 | tf_op jit(solution)/shard_map/out_proj/pallas_call | solution.py:825
  220.1 22.7 %collective-permute-done.25 = bf16[2,256,1536]{2,1,0:T(8,128)(2,1)} collective-permute-done((bf16[2,256,1536]{2,1,0:T(8,128)(2,1)S(1)}, bf16[2,256,1536]{2,1,0:T(8,128)(2,1)}, u32[]{:S(2)}, u32[]{:S(2)}) %collective-permute-start.25) | collective-permute-done | bytes 1572896 | tf_op jit(solution)/shard_map/ppermute | solution.py:1221
  244.8 31.7 %collective-permute-done.24 = bf16[2,256,1536]{2,1,0:T(8,128)(2,1)} collective-permute-done((bf16[2,256,1536]{2,1,0:T(8,128)(2,1)S(1)}, bf16[2,256,1536]{2,1,0:T(8,128)(2,1)}, u32[]{:S(2)}, u32[]{:S(2)}) %collective-permute-start.24) | collective-permute-done | bytes 1572896 | tf_op jit(solution)/shard_map/ppermute | solution.py:1221
  290.2 5.2 mlp.12
  301.5 5.4 mlp.14
  308.8 18.6 %mlp_gram.2 = bf16[1536,1536]{1,0:T(8,128)(2,1)} custom-call(bf16[512,1536]{1,0:T(8,128)(2,1)} %bitcast.128, bf16[512,1536]{1,0:T(8,128)(2,1)} %bitcast.136, bf16[512,1536]{1,0:T(8,128)(2,1)} %bitcast.36.dy.refs_2_, bf16[512,1536]{1,0:T(8,128)(2,1)} %bitcast.38.dy.refs_3_, bf16[512,1536]{1,0:T(8,128)(2,1)} %bitcast.132, bf16[512,1536]{1,0:T(8,128)(2,1)} %bitcast.140, ...), custom_call_target="tpu_custom_call" | custom-call | flops 9663676416 | bytes 23592960 | tf_op jit(solution)/shard_map/mlp_gram/pallas_call | solution.py:1009
  329.8 5.2 mlp.15
  337.9 5.2 sum_nt.15
  346.6 5.3 sum_nt.13
  359.5 5.3 mlp.13
  375.1 18.9 %mlp_gram.3 = bf16[1536,1536]{1,0:T(8,128)(2,1)} custom-call(bf16[512,1536]{1,0:T(8,128)(2,1)} %bitcast.129, bf16[512,1536]{1,0:T(8,128)(2,1)} %bitcast.137, bf16[512,1536]{1,0:T(8,128)(2,1)} %bitcast.36.dy.refs_2_, bf16[512,1536]{1,0:T(8,128)(2,1)} %bitcast.38.dy.refs_3_, bf16[512,1536]{1,0:T(8,128)(2,1)} %bitcast.133, bf16[512,1536]{1,0:T(8,128)(2,1)} %bitcast.141, ...), custom_call_target="tpu_custom_call" | custom-call | flops 9663676416 | bytes 23592960 | tf_op jit(solution)/shard_map/mlp_gram/pallas_call | solution.py:1009
  411.4 10.2 %out_back.1 = (f32[2,256,1536]{2,1,0:T(8,128)}, bf16[2,256,1536]{2,1,0:T(8,128)(2,1)}, bf16[4,2,256,384]{3,2,1,0:T(8,128)(2,1)}, f32[2,8,1536]{2,1,0:T(8,128)}) custom-call(s32[1]{0:T(128)} %bitcast.c_ref, bf16[2,256,1536]{2,1,0:T(8,128)(2,1)} %bitcast.148, bf16[2,256,1536]{2,1,0:T(8,128)(2,1)} %bitcast.41.part_b, f32[2,256,1536]{2,1,0:T(8,128)} %get-tuple-element.64.resid, ...), custom_call_target="tpu_custom_call" | custom-call | flops 2415919104 | bytes 20447232 | tf_op jit(solution)/shard_map/out_back/pallas_call | solution.py:876
  439.9 8.9 %out_gram.1 = bf16[4,2,4,192,384]{4,3,2,1,0:T(8,128)(2,1)S(1)} custom-call(s32[1]{0:T(128)} %bitcast.c_ref, s32[1]{0:T(128)} %bitcast.9.f_ref, bf16[4,2,256,384]{3,2,1,0:T(8,128)(2,1)S(1)} %copy-done.13, bf16[2,2,256,384]{3,2,1,0:T(8,128)(2,1)S(1)} %copy-done.27, bf16[2,2,256,384]{3,2,1,0:T(8,128)(2,1)S(1)} %collective-permute-done.12.m2.m3, ...), custom_call_target="tpu_custom_call" | custom-call | flops 2415919104 | bytes 7864320 | tf_op jit(solution)/shard_map/out_gram/pallas_call | solution.py:1099
  455.9 31.5 %attend_back.1.g.right = bf16[2048,768]{1,0:T(8,128)(2,1)} custom-call(s32[8]{0:T(128)S(1)} %reshape.150.js_ref, s32[1]{0:T(128)} %bitcast.c_ref, bf16[2048,512]{1,0:T(8,128)(2,1)} %get-tuple-element.59.q, bf16[2048,256]{1,0:T(8,128)(2,1)S(1)} %copy-done.74, bf16[2048,512]{1,0:T(8,128)(2,1)} %get-tuple-element.61.v, bf16[4,2,256,384]{3,2,1,0:T(8,128)(2,1)S(1)} %copy-done.13, ...), custom_call_target="tpu_custom_call" | custom-call | flops 20000000000 | bytes 12000000 | tf_op jit(solution)/shard_map/attend_back/pallas_call | solution.py:744
  503.2 19.8 %collective-permute-done.45 = bf16[2,4,192,384]{3,2,1,0:T(8,128)(2,1)S(1)} collective-permute-done((bf16[2,4,192,384]{3,2,1,0:T(8,128)(2,1)S(1)}, bf16[2,4,192,384]{3,2,1,0:T(8,128)(2,1)S(1)}, u32[]{:S(2)}, u32[]{:S(2)}) %collective-permute-start.45) | collective-permute-done | bytes 1179680 | tf_op jit(solution)/shard_map/ppermute | solution.py:1221
  526.1 30.4 %collective-permute-done.37.part_b = bf16[2,256,1536]{2,1,0:T(8,128)(2,1)S(1)} collective-permute-done((bf16[2,256,1536]{2,1,0:T(8,128)(2,1)S(1)}, bf16[2,256,1536]{2,1,0:T(8,128)(2,1)S(1)}, u32[]{:S(2)}, u32[]{:S(2)}) %collective-permute-start.37) | collective-permute-done | bytes 1572896 | tf_op jit(solution)/shard_map/ppermute | solution.py:1221
  567.5 6.8 %split_gram.1 = (bf16[4,192,896]{2,1,0:T(8,128)(2,1)S(1)}, bf16[4,192,896]{2,1,0:T(8,128)(2,1)S(1)}) custom-call(s32[1]{0:T(128)} %bitcast.9.f_ref, bf16[2048,1536]{1,0:T(8,128)(2,1)S(1)} %copy-done.70, bf16[2048,768]{1,0:T(8,128)(2,1)S(1)} %copy-done.68, bf16[1536,128]{1,0:T(8,128)(2,1)S(1)} %add_convert_fusion.8.extra), custom_call_target="tpu_custom_call" | custom-call | flops 4831838208 | bytes 11796480 | tf_op jit(solution)/shard_map/split_gram/pallas_call | solution.py:1051
  576.1 15.3 %collective-permute-done.47 = bf16[2,192,384]{2,1,0:T(8,128)(2,1)S(1)} collective-permute-done((bf16[2,192,384]{2,1,0:T(8,128)(2,1)S(1)}, bf16[2,192,384]{2,1,0:T(8,128)(2,1)S(1)}, u32[]{:S(2)}, u32[]{:S(2)}) %collective-permute-start.47) | collective-permute-done | bytes 294944 | tf_op jit(solution)/shard_map/ppermute | solution.py:1236
  591.5 13.8 %collective-permute-done.38 = bf16[4,192,896]{2,1,0:T(8,128)(2,1)S(1)} collective-permute-done((bf16[4,192,896]{2,1,0:T(8,128)(2,1)S(1)}, bf16[4,192,896]{2,1,0:T(8,128)(2,1)S(1)}, u32[]{:S(2)}, u32[]{:S(2)}) %collective-permute-start.38) | collective-permute-done | bytes 1376288 | tf_op jit(solution)/shard_map/ppermute | solution.py:1236
  608.4 13.9 %collective-permute-done.48 = bf16[192,384]{1,0:T(8,128)(2,1)S(1)} collective-permute-done((bf16[192,384]{1,0:T(8,128)(2,1)S(1)}, bf16[192,384]{1,0:T(8,128)(2,1)S(1)}, u32[]{:S(2)}, u32[]{:S(2)}) %collective-permute-start.48) | collective-permute-done | bytes 147488 | tf_op jit(solution)/shard_map/ppermute | solution.py:1236
  622.6 15.6 %collective-permute-done.39 = bf16[2,192,896]{2,1,0:T(8,128)(2,1)S(1)} collective-permute-done((bf16[2,192,896]{2,1,0:T(8,128)(2,1)S(1)}, bf16[2,192,896]{2,1,0:T(8,128)(2,1)S(1)}, u32[]{:S(2)}, u32[]{:S(2)}) %collective-permute-start.39) | collective-permute-done | bytes 688160 | tf_op jit(solution)/shard_map/ppermute | solution.py:1236
  641.0 6.7 collective-permute-done.40
  649.7 6.4 collective-permute-done.42.s2
  (415 shorter events, 204.7 us)
Async XLA Ops:
  7.2 272.8 %all-gather.3.cloned.1.call-start = ((), (), s32[]{:S(2)}) async-start(), calls=%async_computation.2 | async-start | bytes 5308416 | tf_op jit(solution)/shard_map/all_gather | solution.py:1306
  10.5 316.9 %all-gather.5.cloned.1.call-start = ((), (), s32[]{:S(2)}) async-start(), calls=%async_computation.3 | async-start | bytes 5308416 | tf_op jit(solution)/shard_map/all_gather | solution.py:1306
  23.3 51.6 %collective-permute-start.4 = (bf16[2,256,1536]{2,1,0:T(8,128)(2,1)S(1)}, bf16[2,256,1536]{2,1,0:T(8,128)(2,1)}, u32[]{:S(2)}, u32[]{:S(2)}) collective-permute-start(bf16[2,256,1536]{2,1,0:T(8,128)(2,1)S(1)} %copy-done.23), channel_id=1, source_target_pairs={{0,2},{1,3},{2,0},{3,1},{4,6},{5,7},{6,4},{7,5},{8,10},{9,11},{10,... | collective-permute-start | bytes 4718600 | tf_op jit(solution)/shard_map/ppermute | solution.py:1221
  23.7 123.7 %collective-permute-start.3 = (bf16[2,256,1536]{2,1,0:T(8,128)(2,1)S(1)}, bf16[2,256,1536]{2,1,0:T(8,128)(2,1)}, u32[]{:S(2)}, u32[]{:S(2)}) collective-permute-start(bf16[2,256,1536]{2,1,0:T(8,128)(2,1)S(1)} %copy-done.23), channel_id=1, source_target_pairs={{0,1},{1,0},{2,3},{3,2},{4,5},{5,4},{6,7},{7,6},{8,9},{9,8},{10,11... | collective-permute-start | bytes 4718600 | tf_op jit(solution)/shard_map/ppermute | solution.py:1217
  25.8 409.4 %reduce-scatter.3.cloned.1.call-start = ((), (), s32[]{:S(2)}) async-start(), calls=%async_computation.4 | async-start | bytes 5308416 | tf_op jit(solution)/shard_map/reduce_scatter | solution.py:1364
  26.1 47.3 %collective-permute-start.9 = (bf16[2,192,896]{2,1,0:T(8,128)(2,1)S(1)}, bf16[2,192,896]{2,1,0:T(8,128)(2,1)S(1)}, u32[]{:S(2)}, u32[]{:S(2)}) collective-permute-start(bf16[2,192,896]{2,1,0:T(8,128)(2,1)S(1)} %pad_maximum_fusion.5), channel_id=1, source_target_pairs={{0,16},{4,20},{8,24},{12,28},{16,0},{20,4},{24,8},{28,12},{1,17},{... | collective-permute-start | bytes 2064392 | tf_op jit(solution)/shard_map/ppermute | solution.py:1236
  34.5 40.3 %collective-permute-start.8 = (bf16[192,896]{1,0:T(8,128)(2,1)S(1)}, bf16[192,896]{1,0:T(8,128)(2,1)S(1)}, u32[]{:S(2)}, u32[]{:S(2)}) collective-permute-start(bf16[192,896]{1,0:T(8,128)(2,1)S(1)} %collective-permute-done.7), channel_id=1, source_target_pairs={{0,4},{4,0},{8,12},{12,8},{16,20},{20,16},{24,28},{28,24},{1,5},{5... | collective-permute-start | bytes 1032200 | tf_op jit(solution)/shard_map/ppermute | solution.py:1236
  73.4 29.2 %collective-permute-start.10 = (bf16[2,192,896]{2,1,0:T(8,128)(2,1)S(1)}, bf16[2,192,896]{2,1,0:T(8,128)(2,1)S(1)}, u32[]{:S(2)}, u32[]{:S(2)}) collective-permute-start(bf16[2,192,896]{2,1,0:T(8,128)(2,1)S(1)} %collective-permute-done.9), channel_id=1, source_target_pairs={{0,4},{4,0},{8,12},{12,8},{16,20},{20,16},{24,28},{28,24},{1,5},{5... | collective-permute-start | bytes 2064392 | tf_op jit(solution)/shard_map/ppermute | solution.py:1236
  75.0 72.4 %collective-permute-start.5 = (bf16[2,256,1536]{2,1,0:T(8,128)(2,1)}, bf16[2,256,1536]{2,1,0:T(8,128)(2,1)}, u32[]{:S(2)}, u32[]{:S(2)}) collective-permute-start(bf16[2,256,1536]{2,1,0:T(8,128)(2,1)} %collective-permute-done.4.x2), channel_id=1, source_target_pairs={{0,1},{1,0},{2,3},{3,2},{4,5},{5,4},{6,7},{7,6},{8,9},{9,8},{10,11... | collective-permute-start | bytes 4718600 | tf_op jit(solution)/shard_map/ppermute | solution.py:1217
  112.9 26.1 %collective-permute-start.16 = (bf16[2,192,384]{2,1,0:T(8,128)(2,1)S(1)}, bf16[2,192,384]{2,1,0:T(8,128)(2,1)S(1)}, u32[]{:S(2)}, u32[]{:S(2)}) collective-permute-start(bf16[2,192,384]{2,1,0:T(8,128)(2,1)S(1)} %pad_maximum_fusion.8), channel_id=1, source_target_pairs={{0,16},{4,20},{8,24},{12,28},{16,0},{20,4},{24,8},{28,12},{1,17},{... | collective-permute-start | bytes 884744 | tf_op jit(solution)/shard_map/ppermute | solution.py:1236
  115.6 23.9 %collective-permute-start.15 = (bf16[192,384]{1,0:T(8,128)(2,1)S(1)}, bf16[192,384]{1,0:T(8,128)(2,1)S(1)}, u32[]{:S(2)}, u32[]{:S(2)}) collective-permute-start(bf16[192,384]{1,0:T(8,128)(2,1)S(1)} %collective-permute-done.14), channel_id=1, source_target_pairs={{0,4},{4,0},{8,12},{12,8},{16,20},{20,16},{24,28},{28,24},{1,5},{5... | collective-permute-start | bytes 442376 | tf_op jit(solution)/shard_map/ppermute | solution.py:1236
  145.5 42.6 %collective-permute-start.19 = (bf16[8,192,384]{2,1,0:T(8,128)(2,1)S(1)}, bf16[8,192,384]{2,1,0:T(8,128)(2,1)S(1)}, u32[]{:S(2)}, u32[]{:S(2)}) collective-permute-start(bf16[8,192,384]{2,1,0:T(8,128)(2,1)S(1)} %slice_dynamic-update-slice_fusion.4.p0), channel_id=1, source_target_pairs={{0,2},{1,3},{2,0},{3,1},{4,6},{5,7},{6,4},{7,5},{8,10},{9,11},{10,... | collective-permute-start | bytes 3538952 | tf_op jit(solution)/shard_map/ppermute | solution.py:1221
  190.4 52.4 %collective-permute-start.25 = (bf16[2,256,1536]{2,1,0:T(8,128)(2,1)S(1)}, bf16[2,256,1536]{2,1,0:T(8,128)(2,1)}, u32[]{:S(2)}, u32[]{:S(2)}) collective-permute-start(bf16[2,256,1536]{2,1,0:T(8,128)(2,1)S(1)} %copy-done.10), channel_id=1, source_target_pairs={{0,2},{1,3},{2,0},{3,1},{4,6},{5,7},{6,4},{7,5},{8,10},{9,11},{10,... | collective-permute-start | bytes 4718600 | tf_op jit(solution)/shard_map/ppermute | solution.py:1221
  216.7 59.9 %collective-permute-start.24 = (bf16[2,256,1536]{2,1,0:T(8,128)(2,1)S(1)}, bf16[2,256,1536]{2,1,0:T(8,128)(2,1)}, u32[]{:S(2)}, u32[]{:S(2)}) collective-permute-start(bf16[2,256,1536]{2,1,0:T(8,128)(2,1)S(1)} %get-tuple-element.65), channel_id=1, source_target_pairs={{0,2},{1,3},{2,0},{3,1},{4,6},{5,7},{6,4},{7,5},{8,10},{9,11},{10,... | collective-permute-start | bytes 4718600 | tf_op jit(solution)/shard_map/ppermute | solution.py:1221
  216.8 60.9 %collective-permute-start.22 = (bf16[2,256,1536]{2,1,0:T(8,128)(2,1)S(1)}, bf16[2,256,1536]{2,1,0:T(8,128)(2,1)S(1)}, u32[]{:S(2)}, u32[]{:S(2)}) collective-permute-start(bf16[2,256,1536]{2,1,0:T(8,128)(2,1)S(1)} %copy-done.10), channel_id=1, source_target_pairs={{0,1},{1,0},{2,3},{3,2},{4,5},{5,4},{6,7},{7,6},{8,9},{9,8},{10,11... | collective-permute-start | bytes 4718600 | tf_op jit(solution)/shard_map/ppermute | solution.py:1217
  219.0 59.9 %collective-permute-start.21 = (bf16[2,256,1536]{2,1,0:T(8,128)(2,1)S(1)}, bf16[2,256,1536]{2,1,0:T(8,128)(2,1)S(1)}, u32[]{:S(2)}, u32[]{:S(2)}) collective-permute-start(bf16[2,256,1536]{2,1,0:T(8,128)(2,1)S(1)} %get-tuple-element.65), channel_id=1, source_target_pairs={{0,1},{1,0},{2,3},{3,2},{4,5},{5,4},{6,7},{7,6},{8,9},{9,8},{10,11... | collective-permute-start | bytes 4718600 | tf_op jit(solution)/shard_map/ppermute | solution.py:1217
  242.8 58.7 %collective-permute-start.27 = (bf16[2,256,1536]{2,1,0:T(8,128)(2,1)}, bf16[2,256,1536]{2,1,0:T(8,128)(2,1)}, u32[]{:S(2)}, u32[]{:S(2)}) collective-permute-start(bf16[2,256,1536]{2,1,0:T(8,128)(2,1)} %collective-permute-done.25), channel_id=1, source_target_pairs={{0,1},{1,0},{2,3},{3,2},{4,5},{5,4},{6,7},{7,6},{8,9},{9,8},{10,11... | collective-permute-start | bytes 4718600 | tf_op jit(solution)/shard_map/ppermute | solution.py:1217
  276.5 25.0 %collective-permute-start.26 = (bf16[2,256,1536]{2,1,0:T(8,128)(2,1)}, bf16[2,256,1536]{2,1,0:T(8,128)(2,1)}, u32[]{:S(2)}, u32[]{:S(2)}) collective-permute-start(bf16[2,256,1536]{2,1,0:T(8,128)(2,1)} %collective-permute-done.24), channel_id=1, source_target_pairs={{0,1},{1,0},{2,3},{3,2},{4,5},{5,4},{6,7},{7,6},{8,9},{9,8},{10,11... | collective-permute-start | bytes 4718600 | tf_op jit(solution)/shard_map/ppermute | solution.py:1217
  327.4 230.3 %reduce-scatter.5.cloned.1.call-start = ((), (), s32[]{:S(2)}) async-start(), calls=%async_computation.5 | async-start | bytes 5308416 | tf_op jit(solution)/shard_map/reduce_scatter | solution.py:1365
  343.1 30.3 %collective-permute-start.31 = (bf16[512,1536]{1,0:T(8,128)(2,1)}, bf16[512,1536]{1,0:T(8,128)(2,1)S(1)}, u32[]{:S(2)}, u32[]{:S(2)}) collective-permute-start(bf16[512,1536]{1,0:T(8,128)(2,1)} %sum_nt.15), channel_id=1, source_target_pairs={{0,1},{1,0},{2,3},{3,2},{4,5},{5,4},{6,7},{7,6},{8,9},{9,8},{10,11... | collective-permute-start | bytes 4718600 | tf_op jit(solution)/shard_map/ppermute | solution.py:1217
  351.8 51.7 %collective-permute-start.30 = (bf16[512,1536]{1,0:T(8,128)(2,1)}, bf16[512,1536]{1,0:T(8,128)(2,1)}, u32[]{:S(2)}, u32[]{:S(2)}) collective-permute-start(bf16[512,1536]{1,0:T(8,128)(2,1)} %sum_nt.13), channel_id=1, source_target_pairs={{0,1},{1,0},{2,3},{3,2},{4,5},{5,4},{6,7},{7,6},{8,9},{9,8},{10,11... | collective-permute-start | bytes 4718600 | tf_op jit(solution)/shard_map/ppermute | solution.py:1217
  355.7 76.5 %collective-permute-start.23 = (bf16[512,1536]{1,0:T(8,128)(2,1)}, bf16[512,1536]{1,0:T(8,128)(2,1)}, u32[]{:S(2)}, u32[]{:S(2)}) collective-permute-start(bf16[512,1536]{1,0:T(8,128)(2,1)} %sum_nt.9), channel_id=1, source_target_pairs={{0,1},{1,0},{2,3},{3,2},{4,5},{5,4},{6,7},{7,6},{8,9},{9,8},{10,11... | collective-permute-start | bytes 4718600 | tf_op jit(solution)/shard_map/ppermute | solution.py:1217
  359.0 77.8 %collective-permute-start.28 = (bf16[512,1536]{1,0:T(8,128)(2,1)}, bf16[512,1536]{1,0:T(8,128)(2,1)}, u32[]{:S(2)}, u32[]{:S(2)}) collective-permute-start(bf16[512,1536]{1,0:T(8,128)(2,1)} %sum_nt.11), channel_id=1, source_target_pairs={{0,1},{1,0},{2,3},{3,2},{4,5},{5,4},{6,7},{7,6},{8,9},{9,8},{10,11... | collective-permute-start | bytes 4718600 | tf_op jit(solution)/shard_map/ppermute | solution.py:1217
  375.0 36.4 %collective-permute-start.32 = (bf16[512,1536]{1,0:T(8,128)(2,1)}, bf16[512,1536]{1,0:T(8,128)(2,1)}, u32[]{:S(2)}, u32[]{:S(2)}) collective-permute-start(bf16[512,1536]{1,0:T(8,128)(2,1)} %add_convert_fusion), channel_id=1, source_target_pairs={{0,2},{1,3},{2,0},{3,1},{4,6},{5,7},{6,4},{7,5},{8,10},{9,11},{10,... | collective-permute-start | bytes 4718600 | tf_op jit(solution)/shard_map/ppermute | solution.py:1221
  450.8 42.9 %collective-permute-start.44 = (bf16[2,2,4,192,384]{4,3,2,1,0:T(8,128)(2,1)}, bf16[2,2,4,192,384]{4,3,2,1,0:T(8,128)(2,1)}, u32[]{:S(2)}, u32[]{:S(2)}) collective-permute-start(bf16[2,2,4,192,384]{4,3,2,1,0:T(8,128)(2,1)} %pad_maximum_fusion), channel_id=1, source_target_pairs={{0,1},{1,0},{2,3},{3,2},{4,5},{5,4},{6,7},{7,6},{8,9},{9,8},{10,11... | collective-permute-start | bytes 7077896 | tf_op jit(solution)/shard_map/ppermute | solution.py:1217
  495.2 27.8 %collective-permute-start.45 = (bf16[2,4,192,384]{3,2,1,0:T(8,128)(2,1)S(1)}, bf16[2,4,192,384]{3,2,1,0:T(8,128)(2,1)S(1)}, u32[]{:S(2)}, u32[]{:S(2)}) collective-permute-start(bf16[2,4,192,384]{3,2,1,0:T(8,128)(2,1)S(1)} %fusion.8), channel_id=1, source_target_pairs={{0,2},{1,3},{2,0},{3,1},{4,6},{5,7},{6,4},{7,5},{8,10},{9,11},{10,... | collective-permute-start | bytes 3538952 | tf_op jit(solution)/shard_map/ppermute | solution.py:1221
  500.5 25.2 %collective-permute-start.36 = (bf16[2,256,1536]{2,1,0:T(8,128)(2,1)S(1)}, bf16[2,256,1536]{2,1,0:T(8,128)(2,1)S(1)}, u32[]{:S(2)}, u32[]{:S(2)}) collective-permute-start(bf16[2,256,1536]{2,1,0:T(8,128)(2,1)S(1)} %slice_bitcast_fusion), channel_id=1, source_target_pairs={{0,1},{1,0},{2,3},{3,2},{4,5},{5,4},{6,7},{7,6},{8,9},{9,8},{10,11... | collective-permute-start | bytes 4718600 | tf_op jit(solution)/shard_map/ppermute | solution.py:1217
  501.0 55.6 %collective-permute-start.37 = (bf16[2,256,1536]{2,1,0:T(8,128)(2,1)S(1)}, bf16[2,256,1536]{2,1,0:T(8,128)(2,1)S(1)}, u32[]{:S(2)}, u32[]{:S(2)}) collective-permute-start(bf16[2,256,1536]{2,1,0:T(8,128)(2,1)S(1)} %fusion.1), channel_id=1, source_target_pairs={{0,2},{1,3},{2,0},{3,1},{4,6},{5,7},{6,4},{7,5},{8,10},{9,11},{10,... | collective-permute-start | bytes 4718600 | tf_op jit(solution)/shard_map/ppermute | solution.py:1221
  525.7 48.7 %collective-permute-start.46 = (bf16[4,192,384]{2,1,0:T(8,128)(2,1)}, bf16[4,192,384]{2,1,0:T(8,128)(2,1)}, u32[]{:S(2)}, u32[]{:S(2)}) collective-permute-start(bf16[4,192,384]{2,1,0:T(8,128)(2,1)} %slice_bitcast_fusion.4), channel_id=1, source_target_pairs={{0,4},{4,0},{8,12},{12,8},{16,20},{20,16},{24,28},{28,24},{1,5},{5... | collective-permute-start | bytes 1769480 | tf_op jit(solution)/shard_map/ppermute | solution.py:1236
  574.3 31.0 %collective-permute-start.38 = (bf16[4,192,896]{2,1,0:T(8,128)(2,1)S(1)}, bf16[4,192,896]{2,1,0:T(8,128)(2,1)S(1)}, u32[]{:S(2)}, u32[]{:S(2)}) collective-permute-start(bf16[4,192,896]{2,1,0:T(8,128)(2,1)S(1)} %get-tuple-element.98), channel_id=1, source_target_pairs={{0,4},{4,0},{8,12},{12,8},{16,20},{20,16},{24,28},{28,24},{1,5},{5... | collective-permute-start | bytes 4128776 | tf_op jit(solution)/shard_map/ppermute | solution.py:1236
  575.9 62.7 %collective-permute-start.29 = (bf16[512,1536]{1,0:T(8,128)(2,1)S(1)}, bf16[512,1536]{1,0:T(8,128)(2,1)S(1)}, u32[]{:S(2)}, u32[]{:S(2)}) collective-permute-start(bf16[512,1536]{1,0:T(8,128)(2,1)S(1)} %copy-done.80), channel_id=1, source_target_pairs={{0,2},{1,3},{2,0},{3,1},{4,6},{5,7},{6,4},{7,5},{8,10},{9,11},{10,... | collective-permute-start | bytes 4718600 | tf_op jit(solution)/shard_map/ppermute | solution.py:1221
  605.7 32.5 %collective-permute-start.39 = (bf16[2,192,896]{2,1,0:T(8,128)(2,1)S(1)}, bf16[2,192,896]{2,1,0:T(8,128)(2,1)S(1)}, u32[]{:S(2)}, u32[]{:S(2)}) collective-permute-start(bf16[2,192,896]{2,1,0:T(8,128)(2,1)S(1)} %slice.268), channel_id=1, source_target_pairs={{0,16},{4,20},{8,24},{12,28},{16,0},{20,4},{24,8},{28,12},{1,17},{... | collective-permute-start | bytes 2064392 | tf_op jit(solution)/shard_map/ppermute | solution.py:1236
  (121 other events, 1165.7 us)
Sparse Core Ops, SparseCore 0:
  10.8 128.0 all-gather.2
  141.6 77.0 all-gather.4
  327.5 92.5 reduce-scatter.2
  435.3 92.7 reduce-scatter.4

commit v2 on v1

--- a/solution.py
+++ b/solution.py
@@ -386,6 +386,7 @@
 QH = H // CTX
 KH = KVH // CTX
 BLK = 256
+SHARE = 1.0
 NT = (((1,), (1,)), ((), ()))
 TN = (((0,), (0,)), ((), ()))
 
@@ -411,7 +412,9 @@
 
 
 def cost(flops, nbytes, trans=0):
-    return pl.CostEstimate(flops=int(flops), bytes_accessed=int(nbytes), transcendentals=int(trans))
+    return pl.CostEstimate(
+        flops=int(flops * SHARE), bytes_accessed=int(nbytes * SHARE), transcendentals=int(trans * SHARE)
+    )
 
 
 def packed_columns():
@@ -436,28 +439,20 @@
     return (lax.broadcasted_iota(jnp.int32, (n, n), 0) == src[None, :]).astype(BF)
 
 
-def rms_rows(x, gain):
-    r = lax.rsqrt(jnp.mean(x * x, axis=-1, keepdims=True) + EPSILON)
-    return x * r * gain
-
-
-def qkv_kernel(c_ref, f_ref, x0, x1, x2, x3, gain, w, cos, sin, normed, q, k, v, w_out, xs, ws):
-    @pl.when((pl.program_id(0) == 0) & (pl.program_id(1) == 0))
-    def _():
-        count, rows, _ = w.shape
-        for b in range(count):
-            ws[b * rows : (b + 1) * rows, :] = w[b ^ f_ref[0], :, 0 : ws.shape[1]]
-        w_out[...] = ws[...]
-
+def rms_rows(x):
+    return x * lax.rsqrt(jnp.mean(x * x, axis=-1, keepdims=True) + EPSILON)
+
+
+def qkv_kernel(c_ref, x0, x1, x2, x3, w, cos, sin, normed, q, k, v, xs):
     for d, ref in enumerate((x0, x1, x2, x3)):
 
         @pl.when(pl.program_id(0) == d)
         def _():
             xs[...] = ref[0]
 
-    n = rms_rows(xs[...].astype(F32), gain[...]).astype(BF)
+    n = rms_rows(xs[...].astype(F32)).astype(BF)
     normed[...] = n
-    t = dot_nn(n, ws[...])
+    t = dot_nn(n, w[...])
     y = [t[:, LANES * p : LANES * (p + 1)] for p in range(6)]
     c, s = cos[...], sin[...]
     rot = []
@@ -482,7 +477,7 @@
     v[:, 384:512] = place(((0, 5), (1, 3), (2, 4), (3, 5)))
 
 
-def qkv_call(c, f, xs, gain, w, cos, sin):
+def qkv_call(c, xs, w, cos, sin):
     seqs, tok, width = xs[0].shape
     total = seqs * CTX * tok
     cols = 768
@@ -490,47 +485,39 @@
     def own(d):
         return pl.BlockSpec(
             (1, tok, width),
-            lambda i, s, c, f: (jnp.where(i == d, s, jnp.where(i < d, 0, seqs - 1)), 0, 0),
+            lambda i, s, c: (jnp.where(i == d, s, jnp.where(i < d, 0, seqs - 1)), 0, 0),
         )
 
     def rows(n):
-        return pl.BlockSpec((tok, n), lambda i, s, c, f: (s * CTX + (i ^ c[0]), 0))
+        return pl.BlockSpec((tok, n), lambda i, s, c: (s * CTX + (i ^ c[0]), 0))
 
     return pl.pallas_call(
         qkv_kernel,
         grid_spec=pltpu.PrefetchScalarGridSpec(
-            num_scalar_prefetch=2,
+            num_scalar_prefetch=1,
             grid=(CTX, seqs),
             in_specs=[
                 own(0),
                 own(1),
                 own(2),
                 own(3),
-                pl.BlockSpec((1, width), lambda i, s, c, f: (0, 0)),
-                pl.BlockSpec(w.shape, lambda i, s, c, f: (0, 0, 0)),
+                pl.BlockSpec((width, cols), lambda i, s, c: (0, 0)),
                 rows(LANES),
                 rows(LANES),
             ],
-            out_specs=[
-                rows(width),
-                rows(512),
-                rows(256),
-                rows(512),
-                pl.BlockSpec((width, cols), lambda i, s, c, f: (0, 0)),
-            ],
-            scratch_shapes=[pltpu.VMEM((tok, width), BF), pltpu.VMEM((width, cols), BF)],
+            out_specs=[rows(width), rows(512), rows(256), rows(512)],
+            scratch_shapes=[pltpu.VMEM((tok, width), BF)],
         ),
         out_shape=[
             jax.ShapeDtypeStruct((total, width), BF),
             jax.ShapeDtypeStruct((total, 512), BF),
             jax.ShapeDtypeStruct((total, 256), BF),
             jax.ShapeDtypeStruct((total, 512), BF),
-            jax.ShapeDtypeStruct((width, cols), BF),
         ],
-        compiler_params=params(48, ("arbitrary", "arbitrary")),
-        cost_estimate=cost(2 * total * width * 768, total * width * 4 + width * 768 * 4 + total * 3584),
+        compiler_params=params(40, ("arbitrary", "arbitrary")),
+        cost_estimate=cost(2 * total * width * 768, total * width * 4 + width * 768 * 2 + total * 3584),
         name="qkv",
-    )(c, f, *xs, gain, w, cos, sin)
+    )(c, *xs, w, cos, sin)
 
 
 def head_masks(rows):
@@ -804,17 +791,17 @@
     )(c, f, *parts)
 
 
-def out_kernel(c_ref, x, m0, m1, m2, m3, w, gain, resid, normed):
+def out_kernel(c_ref, x, m0, m1, m2, m3, w, resid, normed):
     c = c_ref[0]
     acc = x[0].astype(F32)
     for d, ref in enumerate((m0, m1, m2, m3)):
         rows = pl.ds(pl.multiple_of((d ^ c) * (QH * HD), QH * HD), QH * HD)
         acc = acc + dot_nn(ref[0, 0], w[rows, :])
     resid[0] = acc
-    normed[0] = rms_rows(acc, gain[...]).astype(BF)
-
-
-def out_call(c, x, mixed, r1, r2, w, gain):
+    normed[0] = rms_rows(acc).astype(BF)
+
+
+def out_call(c, x, mixed, r1, r2, w):
     seqs, tok, width = x.shape
     inner_w = QH * HD
 
@@ -834,7 +821,6 @@
                 slot(0),
                 slot(1),
                 pl.BlockSpec((H * HD, width), lambda s, c: (0, 0)),
-                pl.BlockSpec((1, width), lambda s, c: (0, 0)),
             ],
             out_specs=[tile, tile],
         ),
@@ -845,31 +831,27 @@
         compiler_params=params(48, ("arbitrary",)),
         cost_estimate=cost(2 * seqs * tok * width * width, width * width * 2 + seqs * tok * width * 10),
         name="out_proj",
-    )(c, x, mixed, r1, r2, r2, w, gain)
-
-
-def rms_back(v, gain, dy):
+    )(c, x, mixed, r1, r2, r2, w)
+
+
+def rms_back(v, dyg):
     r = lax.rsqrt(jnp.mean(v * v, axis=-1, keepdims=True) + EPSILON)
-    dyg = dy * gain
-    inner_sum = jnp.mean(dyg * v, axis=-1, keepdims=True)
-    return r * dyg - v * (r * r * r * inner_sum), dy * v * r
-
-
-def out_back_kernel(c_ref, part_a, part_b, resid, gain, dy, w, dresid, dattn, dmixed, dgain):
+    return r * dyg - v * (r * r * r * jnp.mean(dyg * v, axis=-1, keepdims=True))
+
+
+def out_back_kernel(c_ref, part_a, part_b, resid, dy, w, dresid, dattn, dmixed):
     c = c_ref[0]
     dn = part_a[0].astype(F32) + part_b[0].astype(F32)
-    dr, dg = rms_back(resid[0], gain[...], dn)
-    total = dy[0].astype(F32) + dr
+    total = dy[0].astype(F32) + rms_back(resid[0], dn)
     dresid[0] = total
     low = total.astype(BF)
     dattn[0] = low
-    dgain[0] = jnp.broadcast_to(jnp.sum(dg, axis=0, keepdims=True), dgain.shape[1:])
     for d in range(CTX):
         rows = pl.ds(pl.multiple_of((d ^ c) * (QH * HD), QH * HD), QH * HD)
         dmixed[d, 0] = dot_nt(low, w[rows, :]).astype(BF)
 
 
-def out_back_call(c, part_a, part_b, resid, gain, dy, w):
+def out_back_call(c, part_a, part_b, resid, dy, w):
     seqs, tok, width = dy.shape
     inner_w = QH * HD
     tile = pl.BlockSpec((1, tok, width), lambda s, c: (s, 0, 0))
@@ -882,7 +864,6 @@
                 tile,
                 tile,
                 tile,
-                pl.BlockSpec((1, width), lambda s, c: (0, 0)),
                 tile,
                 pl.BlockSpec((H * HD, width), lambda s, c: (0, 0)),
             ],
@@ -890,19 +871,17 @@
                 tile,
                 tile,
                 pl.BlockSpec((CTX, 1, tok, inner_w), lambda s, c: (0, s, 0, 0)),
-                pl.BlockSpec((1, 8, width), lambda s, c: (s, 0, 0)),
             ],
         ),
         out_shape=[
             jax.ShapeDtypeStruct((seqs, tok, width), F32),
             jax.ShapeDtypeStruct((seqs, tok, width), BF),
             jax.ShapeDtypeStruct((CTX, seqs, tok, inner_w), BF),
-            jax.ShapeDtypeStruct((seqs, 8, width), F32),
         ],
         compiler_params=params(56, ("arbitrary",)),
         cost_estimate=cost(2 * seqs * tok * width * width, width * width * 2 + seqs * tok * width * 20),
         name="out_back",
-    )(c, part_a, part_b, resid, gain, dy, w)
+    )(c, part_a, part_b, resid, dy, w)
 
 
 def mlp_kernel(n2, dy, wg, wu, wd, hidden, grads):
@@ -1021,50 +1000,26 @@
     )(*dys, *n2s, *hid, *gu)
 
 
-def split_gram_kernel(f_ref, left, right, extra, mine, theirs):
-    acc = dot_tn(left[...], right[...]).astype(BF)
-    rows = mine.shape[1]
-    k = right.shape[1]
-    side = f_ref[0] % 2
-
-    @pl.when(side == 0)
-    def _():
-        mine[0, :, :k] = acc[:rows]
-        theirs[0, :, :k] = acc[rows:]
-        mine[0, :, k:] = extra[:rows]
-        theirs[0, :, k:] = extra[rows:]
-
-    @pl.when(side != 0)
-    def _():
-        mine[0, :, :k] = acc[rows:]
-        theirs[0, :, :k] = acc[:rows]
-        mine[0, :, k:] = extra[rows:]
-        theirs[0, :, k:] = extra[:rows]
-
-
-def split_gram_call(f, left, right, extra):
-    tokens, m = left.shape
-    k, e = right.shape[1], extra.shape[1]
-    pair = m // 4
-    out = pl.BlockSpec((1, pair // 2, k + e), lambda z, f: (z ^ (f[0] // 2), 0, 0))
-    shape = jax.ShapeDtypeStruct((4, pair // 2, k + e), BF)
+def gram_kernel(left, right, out):
+    out[...] = dot_tn(left[...], right[...]).astype(out.dtype)
+
+
+def gram_call(left, right, tile_m, tile_n):
+    rows, m = left.shape
+    n = right.shape[1]
     return pl.pallas_call(
-        split_gram_kernel,
-        grid_spec=pltpu.PrefetchScalarGridSpec(
-            num_scalar_prefetch=1,
-            grid=(4,),
-            in_specs=[
-                pl.BlockSpec((tokens, pair), lambda z, f: (0, z)),
-                pl.BlockSpec((tokens, k), lambda z, f: (0, 0)),
-                pl.BlockSpec((pair, e), lambda z, f: (z, 0)),
-            ],
-            out_specs=[out, out],
-        ),
-        out_shape=[shape, shape],
-        compiler_params=params(40, ("arbitrary",)),
-        cost_estimate=cost(2 * tokens * m * k, tokens * (m + k) * 2 + m * k * 2),
-        name="split_gram",
-    )(f, left, right, extra)
+        gram_kernel,
+        grid=(n // tile_n, m // tile_m),
+        in_specs=[
+            pl.BlockSpec((rows, tile_m), lambda j, i: (0, i)),
+            pl.BlockSpec((rows, tile_n), lambda j, i: (0, j)),
+        ],
+        out_specs=pl.BlockSpec((tile_m, tile_n), lambda j, i: (i, j)),
+        out_shape=jax.ShapeDtypeStruct((m, n), BF),
+        compiler_params=params(40, ("arbitrary", "arbitrary")),
+        cost_estimate=cost(2 * rows * m * n, rows * (m + n) * 2 + m * n * 2),
+        name="gram",
+    )(left, right)
 
 
 def out_gram_kernel(c_ref, f_ref, m0, m1, m2, m3, dattn, out):
@@ -1119,10 +1074,11 @@
     )(c, f, mixed, r1, r2, r2, dattn)
 
 
-def unpack_kernel(c_ref, s0, s1, s2, s3, perm, o0, o1, o2, o3, gq, gk, gv, gg, go):
+def unpack_kernel(c_ref, s0, s1, s2, s3, perm, o0, o1, o2, o3, wq, wk, wv, gain, gq, gk, gv, gg, gm, go):
     c = c_ref[0]
     qw, kw = QH * HD, KH * HD
     n = perm.shape[0]
+    g = gain[...]
     for b in range(CTX):
         for d, (ref, out) in enumerate(((s0, o0), (s1, o1), (s2, o2), (s3, o3))):
 
@@ -1134,30 +1090,35 @@
                 gv[:, b * kw : (b + 1) * kw] = flat[:, qw + kw :]
                 go[:, b * qw : (b + 1) * qw] = out[...].astype(F32)
 
-    gg[...] = (
+    total = jnp.zeros_like(g)
+    for grad, w in ((gq, wq), (gk, wk), (gv, wv)):
+        total = total + jnp.sum(grad[...] * w[...].astype(F32), axis=-1, keepdims=True)
+        grad[...] = grad[...] * g
+    gg[...] = total
+    gm[...] = (
         s0[:, n:].astype(F32) + s1[:, n:].astype(F32) + s2[:, n:].astype(F32) + s3[:, n:].astype(F32)
-    )
-
-
-def unpack_call(c, parts, perm, outs):
+    )[:, 0:1]
+
+
+def unpack_call(c, parts, perm, outs, wq, wk, wv, gain):
     rows = parts[0].shape[0]
-    extra = parts[0].shape[1] - perm.shape[0]
     vm = pl.BlockSpec(memory_space=pltpu.VMEM)
     return pl.pallas_call(
         unpack_kernel,
-        in_specs=[pl.BlockSpec(memory_space=pltpu.SMEM)] + [vm] * 9,
-        out_specs=[vm] * 5,
+        in_specs=[pl.BlockSpec(memory_space=pltpu.SMEM)] + [vm] * 13,
+        out_specs=[vm] * 6,
         out_shape=[
             jax.ShapeDtypeStruct((rows, H * HD), F32),
             jax.ShapeDtypeStruct((rows, KVH * HD), F32),
             jax.ShapeDtypeStruct((rows, KVH * HD), F32),
-            jax.ShapeDtypeStruct((rows, extra), F32),
+            jax.ShapeDtypeStruct((rows, 1), F32),
+            jax.ShapeDtypeStruct((rows, 1), F32),
             jax.ShapeDtypeStruct((rows, CTX * outs[0].shape[1]), F32),
         ],
         compiler_params=pltpu.CompilerParams(vmem_limit_bytes=40 << 20),
         cost_estimate=cost(1e9, 1e7),
         name="unpack",
-    )(c, *parts, perm, *outs)
+    )(c, *parts, perm, *outs, wq, wk, wv, gain)
 
 
 def qkv_back_kernel(c_ref, g, w, out):
@@ -1184,29 +1145,24 @@
     )(c, grads, w)
 
 
-def final_kernel(part_a, part_b, x, gain, dresid, out, dgain):
+def final_kernel(part_a, part_b, x, dresid, out):
     dn = part_a[0].astype(F32) + part_b[0].astype(F32)
-    dx, dg = rms_back(x[0].astype(F32), gain[...], dn)
-    out[0] = dresid[0] + dx
-    dgain[0] = jnp.broadcast_to(jnp.sum(dg, axis=0, keepdims=True), dgain.shape[1:])
-
-
-def final_call(part_a, part_b, x, gain, dresid):
+    out[0] = dresid[0] + rms_back(x[0].astype(F32), dn)
+
+
+def final_call(part_a, part_b, x, dresid):
     seqs, tok, width = x.shape
     tile = pl.BlockSpec((1, tok, width), lambda s: (s, 0, 0))
     return pl.pallas_call(
         final_kernel,
         grid=(seqs,),
-        in_specs=[tile, tile, tile, pl.BlockSpec((1, width), lambda s: (0, 0)), tile],
-        out_specs=[tile, pl.BlockSpec((1, 8, width), lambda s: (s, 0, 0))],
-        out_shape=[
-            jax.ShapeDtypeStruct((seqs, tok, width), F32),
-            jax.ShapeDtypeStruct((seqs, 8, width), F32),
-        ],
+        in_specs=[tile] * 4,
+        out_specs=tile,
+        out_shape=jax.ShapeDtypeStruct((seqs, tok, width), F32),
         compiler_params=params(40, ("arbitrary",)),
         cost_estimate=cost(20 * seqs * tok * width, 14 * seqs * tok * width),
         name="final",
-    )(part_a, part_b, x, gain, dresid)
+    )(part_a, part_b, x, dresid)
 
 
 CORE = [(i, i ^ 1) for i in range(CTX)]
@@ -1278,10 +1234,11 @@
     c = ctx.astype(jnp.int32).reshape(1)
 
     segs = gather_blocks(segments)
-    xs = gather_blocks(after(tokens, *segs))
-    dys = gather_blocks(after(cotangent, *xs))
+    xs = gather_blocks(tokens)
 
     perm = pack_matrix()
+    fsdp = lax.axis_index("fsdp").astype(jnp.int32).reshape(1)
+    col_a, col_m = gain_attn.astype(F32)[:, None], gain_mlp.astype(F32)[:, None]
     shard = jnp.concatenate(
         [
             lax.dynamic_slice_in_dim(w_query, ctx * (QH * HD), QH * HD, 1),
@@ -1290,30 +1247,29 @@
         ],
         axis=1,
     )
-    shard = jnp.dot(shard, perm, preferred_element_type=F32).astype(BF)
-    gains = jnp.pad(jnp.stack([gain_attn, gain_mlp], axis=1), ((0, 0), (0, LANES - 2)))
-    shard = jnp.concatenate([shard, gains], axis=1)
-    fsdp = lax.axis_index("fsdp").astype(jnp.int32).reshape(1)
-    w_qkv = gather_fsdp(shard)
+    shard = jnp.dot(shard, perm, preferred_element_type=F32)
+    shard = (shard * col_a).astype(BF)
+    w_qkv = lax.all_gather(shard, "fsdp", axis=0, tiled=True)
+    quarter = width // CTX
+    out_part = gather_fsdp(lax.dynamic_slice_in_dim(w_out, ctx * quarter, quarter, 1))
+    dys = gather_blocks(after(cotangent, xs[2]))
+    out_parts = gather_blocks(out_part)
+    w_out_full = assemble_call(c, fsdp, out_parts)
     down_t = jnp.transpose(w_down)
     ff = w_gate.shape[1] // 2
     w_parts = []
     for n in range(2):
         cols = slice(n * ff, (n + 1) * ff)
-        part = jnp.concatenate([w_gate[:, cols], w_up[:, cols], down_t[:, cols]], axis=1)
-        if n:
-            part = after(part, *segs)
+        part = jnp.concatenate(
+            [
+                (w_gate[:, cols].astype(F32) * col_m).astype(BF),
+                (w_up[:, cols].astype(F32) * col_m).astype(BF),
+                down_t[:, cols],
+            ],
+            axis=1,
+        )
+        part = after(part, *(segs if n else [shard]))
         w_parts.append(lax.all_gather(part, "fsdp", axis=0, tiled=True))
-    gain_cols = w_qkv[:, :, qkv_w : qkv_w + 2]
-    gain_cols = jnp.concatenate(
-        [lax.dynamic_index_in_dim(gain_cols, b ^ fsdp[0], 0, keepdims=False) for b in range(8)], axis=0
-    )
-    gain_rows = jnp.transpose(gain_cols).astype(F32)
-    gain_a, gain_m = gain_rows[0:1], gain_rows[1:2]
-    quarter = width // CTX
-    out_part = gather_fsdp(after(lax.dynamic_slice_in_dim(w_out, ctx * quarter, quarter, 1), w_qkv))
-    out_parts = gather_blocks(out_part)
-    w_out_full = assemble_call(c, fsdp, out_parts)
 
     seg_blocks = jnp.stack(segs)
     whole_seg = jnp.concatenate(
@@ -1334,70 +1290,90 @@
     low_block = (first[:, ::BLK] // BLK).reshape(seqs * CTX).astype(jnp.int32)
     first_rows = first.reshape(seqs, CTX, 1, BLK)
 
-    normed, q, k, v, w_packed = qkv_call(c, fsdp, xs, gain_a, w_qkv, cos, sin)
-    mixed, lse = attend_call(c, low_block, q, k, v, first_rows, seqs, length)
+    normed, q, k, v = qkv_call(c, xs, w_qkv, cos, sin)
+    mixed, lse = attend_call(c, low_block, after(q, dys[2]), k, v, first_rows, seqs, length)
     r1 = swap_core(jnp.stack([mixed[1], mixed[3]]))
     r2 = swap_row(jnp.stack([mixed[2], r1[1]]))
-    resid, normed_two = out_call(c, tokens, mixed, r1, r2, w_out_full, gain_m)
+    resid, normed_two = out_call(c, tokens, mixed, r1, r2, w_out_full)
 
     n2s = [n.reshape(rows, width) for n in gather_blocks(normed_two)]
     dys = [d.reshape(rows, width) for d in dys]
-    hiddens, grads, shares = [], [], []
-    for w in w_parts:
-        pairs = [mlp_call(n2s[d], dys[d], w) for d in range(CTX)]
-        hiddens.append([p[0] for p in pairs])
-        grads.append([p[1] for p in pairs])
-        gram = mlp_gram_call(dys, n2s, hiddens[-1], grads[-1], 512)
-        shares.append(gram)
+    first_pairs = [mlp_call(n2s[d], dys[d], w_parts[0]) for d in (0, 1)]
+    n2s[2] = after(n2s[2], first_pairs[0][0], first_pairs[1][0])
+    n2s[3] = after(n2s[3], first_pairs[0][0], first_pairs[1][0])
+    first_pairs += [mlp_call(n2s[d], dys[d], w_parts[0]) for d in (2, 3)]
+    share_one = mlp_gram_call(dys, n2s, [p[0] for p in first_pairs], [p[1] for p in first_pairs], 768)
+    s_one = lax.psum_scatter(share_one, "fsdp", scatter_dimension=0, tiled=True)
+    second_pairs = [None] * CTX
 
     def back_rows(d):
-        terms = [(grads[n][d], slot, w_parts[n], slot) for n in range(2) for slot in range(2)]
+        terms = [(pairs[d][1], slot, w, slot) for pairs, w in zip((first_pairs, second_pairs), w_parts) for slot in range(2)]
         return sum_nt_call(terms, 512)
 
-    def down_rows(d):
-        return sum_nt_call([(hiddens[n][d], None, w_parts[n], 2) for n in range(2)], 512)
-
-    dn3, dn2, dn1, dn0 = [back_rows(d) for d in (3, 2, 1, 0)]
-    dn2 = add_low(dn2, swap_core(dn3))
+    def down_rows(d, dep):
+        halves = (after(first_pairs[d][0], dep), second_pairs[d][0])
+        return sum_nt_call([(h, None, w, 2) for h, w in zip(halves, w_parts)], 512)
+
+    n2_gate = after(n2s[3], share_one)
+    for d in (3, 2):
+        second_pairs[d] = mlp_call(n2_gate if d == 3 else n2s[d], dys[d], w_parts[1])
+    dn2 = add_low(back_rows(2), swap_core(back_rows(3)))
     dn_b = swap_row(dn2)
-    dn_a = add_low(dn0, swap_core(dn1))
-    s_one = lax.psum_scatter(shares[0], "fsdp", scatter_dimension=0, tiled=True)
-    s_two = lax.psum_scatter(after(shares[1], s_one), "fsdp", scatter_dimension=0, tiled=True)
-    dn_b = after(dn_b, dn_a, *shares)
-    dresid, dattn, dmixed, dgain_m = out_back_call(
-        c, dn_a.reshape(tokens.shape), dn_b.reshape(tokens.shape), resid, gain_m, cotangent, w_out_full
+    for d in (1, 0):
+        second_pairs[d] = mlp_call(after(n2s[d], dn2), dys[d], w_parts[1])
+    dn_a = add_low(back_rows(0), swap_core(back_rows(1)))
+    share_two = mlp_gram_call(dys, n2s, [p[0] for p in second_pairs], [p[1] for p in second_pairs], 768)
+    s_two = lax.psum_scatter(share_two, "fsdp", scatter_dimension=0, tiled=True)
+    dn_b = after(dn_b, dn_a, share_two)
+    dresid, dattn, dmixed = out_back_call(
+        c, dn_a.reshape(tokens.shape), dn_b.reshape(tokens.shape), resid, cotangent, w_out_full
     )
 
     b1 = swap_core(jnp.stack([dmixed[1], dmixed[3]]))
-    b2 = swap_row(jnp.stack([dmixed[2], b1[1]]))
-    g_out = out_gram_call(c, fsdp, mixed, r1, r2, dattn.reshape(rows, width))
+    b2_send = jnp.stack([dmixed[2], b1[1]])
+    b2 = swap_row(b2_send)
+    g_out = out_gram_call(c, fsdp, mixed, r1, r2, after(dattn, b2_send).reshape(rows, width))
     got = swap_core(jnp.stack([g_out[1], g_out[3]]))
-    downs = [down_rows(d) for d in range(CTX)]
+    g_send = add_low(g_out[2], got[1])
+    got_row = swap_row(g_send)
+    b2 = after(b2, g_send, s_one)
+    dqkv = attend_back_call(
+        c, low_block, q, k, v, mixed, dmixed, b1[0], b2, lse, first_rows, cos, sin, seqs, length
+    )
+
+    g_qkv = gram_call(normed, dqkv, 768, 768)
+    dqkv_b = after(dqkv, g_qkv)
+    far = qkv_back_call(c, dqkv_b, w_qkv, seqs, 2)
+    dx2 = add_low(far[0], swap_core(far[1]))
+    dx_b = swap_row(dx2)
+    near = qkv_back_call(c, dqkv_b, w_qkv, seqs, 0)
+    dx_a = add_low(near[0], swap_core(near[1]))
+    g_out = add_low(add_low(g_out[0], got[0]), after(got_row, dx2))
+    s_out = reduce_fsdp(g_out[0], g_out[1])
+    downs = [down_rows(d, dx2) for d in range(CTX)]
     down2 = add_low(downs[2], swap_core(downs[3]))
     down_b = swap_row(down2)
     down_a = add_low(downs[0], swap_core(downs[1]))
-    got_row = swap_row(add_low(g_out[2], got[1]))
-    g_out = add_low(add_low(g_out[0], got[0]), got_row)
-    b2 = after(b2, down2, down_a, s_one)
-    dqkv = attend_back_call(
-        c, low_block, q, k, v, mixed, dmixed, b1[0], b2, lse, first_rows, cos, sin, seqs, length
-    )
-    s_out = reduce_fsdp(g_out[0], g_out[1])
-
-    far = qkv_back_call(c, dqkv, w_packed, seqs, 2)
-    dx2 = add_low(far[0], swap_core(far[1]))
-    dx_b = swap_row(dx2)
-    gain_m_col = jnp.pad(jnp.sum(dgain_m[:, 0], axis=0)[:, None], ((0, 0), (1, LANES - 2)))
-    near = qkv_back_call(c, after(dqkv, dx2), w_packed, seqs, 0)
-    dx_a = add_low(near[0], swap_core(near[1]))
     output = (
         resid + down_a.astype(F32).reshape(resid.shape) + down_b.astype(F32).reshape(resid.shape)
     ).astype(BF)
-    grad_tokens, dgain_a = final_call(dx_a, after(dx_b, s_two), tokens, gain_a, dresid)
-    gain_grads = jnp.pad(jnp.sum(dgain_a[:, 0], axis=0)[:, None], ((0, 0), (0, LANES - 1))) + gain_m_col
-    s_qkv = reduce_fsdp(*split_gram_call(fsdp, normed, dqkv, gain_grads.astype(BF)))
-    g_query, g_key, g_value, g_gain, g_w_out = unpack_call(
-        c, gather_blocks(s_qkv), perm, gather_blocks(s_out)
+    grad_tokens = final_call(dx_a, after(dx_b, s_two), tokens, dresid)
+    s_qkv = lax.psum_scatter(g_qkv, "fsdp", scatter_dimension=0, tiled=True)
+    s_down, s_gate, s_up = [
+        jnp.concatenate([s[:, n * ff : (n + 1) * ff] for s in (s_one, s_two)], axis=1).astype(F32)
+        for n in range(3)
+    ]
+    part_m = jnp.sum(s_gate * w_gate.astype(F32) + s_up * w_up.astype(F32), axis=1, keepdims=True)
+    part_m = jnp.broadcast_to(part_m, (part_m.shape[0], LANES)).astype(BF)
+    g_query, g_key, g_value, g_gain_a, g_gain_m, g_w_out = unpack_call(
+        c,
+        gather_blocks(jnp.concatenate([s_qkv, part_m], axis=1)),
+        perm,
+        gather_blocks(s_out),
+        w_query,
+        w_key,
+        w_value,
+        col_a,
     )
     return (
         output,
@@ -1406,11 +1382,11 @@
         g_key,
         g_value,
         g_w_out,
-        jnp.concatenate([s[:, ff : 2 * ff] for s in (s_one, s_two)], axis=1).astype(F32),
-        jnp.concatenate([s[:, 2 * ff :] for s in (s_one, s_two)], axis=1).astype(F32),
-        jnp.transpose(jnp.concatenate([s[:, :ff] for s in (s_one, s_two)], axis=1)).astype(F32),
-        g_gain[:, 0],
-        g_gain[:, 1],
+        s_gate * col_m,
+        s_up * col_m,
+        jnp.transpose(s_down),
+        g_gain_a[:, 0],
+        g_gain_m[:, 0],
     )
 
 

time: 677 us -> 568 us (0.84)
  waiting for transfers between devices: 288 us -> 181 us
  starting transfers between devices: 52.4 us -> 37.6 us
    ppermute x16 -> x8, waiting for transfers between devices: 150 us -> 32.4 us  [swap_fsdp(): return lax.ppermute(x, 'fsdp', [(i, i ^ bit) for i in range(size)])]
    ppermute x16 -> x8, starting transfers between devices: 19.8 us -> 8.21 us  [swap_fsdp(): return lax.ppermute(x, 'fsdp', [(i, i ^ bit) for i in range(size)])]
    unnamed x210 -> x208, local copies, waits for them, and re-layouts: 46.9 us -> 56.3 us
    ppermute x23, starting transfers between devices: 25.9 us -> 18.7 us  [swap_core(): return lax.ppermute(x, 'context', CORE)]
    convert_element_type x14 -> x11, other arithmetic: 16.8 us -> 18.8 us  [add_low(): return (a.astype(F32) + b.astype(F32)).astype(BF)]
  transfers between devices with their start and end apart: 56 -> 50, of which waited for: 21 -> 19; matrix products, arithmetic and copies ran while one was open for 8% -> 9% of each run, Pallas kernels for 32% -> 38%
where the time goes in v2:
time: 568 us; the launch traced here: 565 us
  Pallas kernels  223 us (39%)
  waiting for transfers between devices  181 us (32%)
  local copies, waits for them, and re-layouts  66.5 us (12%)
  other arithmetic  39.1 us (7%)
  starting transfers between devices  37.6 us (7%)
  between operations  15.6 us (3%)
    ppermute x13, waiting for transfers between devices, swap_row(): return lax.ppermute(x, 'context', ROW)  134 us
    unnamed x208, local copies, waits for them, and re-layouts  56.3 us
    pallas_call x8, Pallas kernels, mlp_call(): pl.pallas_call(mlp_kernel, grid=(steps,), in_specs=[full, full, pl.BlockS...  40.3 us
    pallas_call x2, Pallas kernels, mlp_gram_call(): pl.pallas_call(functools.partial(mlp_gram_kernel, count), grid=(3, m // t...  36.1 us
    ppermute x8, waiting for transfers between devices, swap_fsdp(): return lax.ppermute(x, 'fsdp', [(i, i ^ bit) for i in range(size)])  32.4 us
    pallas_call x1, Pallas kernels, attend_back_call(): pl.pallas_call(attend_back_kernel, grid_spec=pltpu.PrefetchScalarGridSpec...  31.2 us
    pallas_call x8, Pallas kernels, sum_nt_call(): pl.pallas_call(functools.partial(sum_nt_kernel, tuple((t[1] for t in term...  30.2 us
    convert_element_type x11, other arithmetic, add_low(): return (a.astype(F32) + b.astype(F32)).astype(BF)  18.8 us
  transfers between devices with their start and end apart: 50, of which 19 were waited for; matrix products, arithmetic and copies ran while one was open for 9% of the time, Pallas kernels for 38%

profile of v2, /device:TPU:1, one launch (start us, length us, event | category | flops | bytes accessed | tf_op | source)
XLA Modules:
  0.0 564.8 jit_solution(14675197650093815598)
XLA Ops:
  25.5 5.4 multiply_sine_fusion
  33.5 22.4 %collective-permute-done.4.x2 = bf16[2,256,1536]{2,1,0:T(8,128)(2,1)} collective-permute-done((bf16[2,256,1536]{2,1,0:T(8,128)(2,1)}, bf16[2,256,1536]{2,1,0:T(8,128)(2,1)}, u32[]{:S(2)}, u32[]{:S(2)}) %collective-permute-start.4) | collective-permute-done | bytes 1572896 | tf_op jit(solution)/shard_map/ppermute | solution.py:1177
  61.0 9.5 %collective-permute-done.13 = bf16[2,192,384]{2,1,0:T(8,128)(2,1)S(1)} collective-permute-done((bf16[2,192,384]{2,1,0:T(8,128)(2,1)S(1)}, bf16[2,192,384]{2,1,0:T(8,128)(2,1)S(1)}, u32[]{:S(2)}, u32[]{:S(2)}) %collective-permute-start.13) | collective-permute-done | bytes 294944 | tf_op jit(solution)/shard_map/ppermute | solution.py:1192
  79.0 13.1 %qkv.1 = (bf16[2048,1536]{1,0:T(8,128)(2,1)}, bf16[2048,512]{1,0:T(8,128)(2,1)S(1)}, bf16[2048,256]{1,0:T(8,128)(2,1)S(1)}, bf16[2048,512]{1,0:T(8,128)(2,1)S(1)}) custom-call(s32[1]{0:T(128)} %bitcast.c_ref, bf16[2,256,1536]{2,1,0:T(8,128)(2,1)} %x.5, bf16[2,256,1536]{2,1,0:T(8,128)(2,1)} %collective-permute-done.3.x1, ...), custom_call_target="tpu_custom_call" | custom-call | flops 4831838208 | bytes 22282240 | tf_op jit(solution)/shard_map/qkv/pallas_call | solution.py:494
  95.2 18.0 %attend.1 = (bf16[4,2,256,384]{3,2,1,0:T(8,128)(2,1)S(1)}, f32[2,4,8,256]{3,2,1,0:T(8,128)S(1)}) custom-call(s32[8]{0:T(128)S(1)} %reshape.151.js_ref, s32[1]{0:T(128)} %bitcast.c_ref, bf16[2048,512]{1,0:T(8,128)(2,1)S(1)} %get-tuple-element.65.q, bf16[2048,256]{1,0:T(8,128)(2,1)S(1)} %get-tuple-element.66.k, bf16[2048,512]{1,0:T(8,128)(2,1)S(1)} %get-tuple-element.67.v, ...), custom_call_target="tpu_custom_call" | custom-call | flops 6000000000 | bytes 8000000 | tf_op jit(solution)/shard_map/attend/pallas_call | solution.py:592
  124.4 5.5 assemble.1.w
  132.0 10.2 %collective-permute-done.8.m2.m3 = bf16[2,2,256,384]{3,2,1,0:T(8,128)(2,1)S(1)} collective-permute-done((bf16[2,2,256,384]{3,2,1,0:T(8,128)(2,1)}, bf16[2,2,256,384]{3,2,1,0:T(8,128)(2,1)S(1)}, u32[]{:S(2)}, u32[]{:S(2)}) %collective-permute-start.8) | collective-permute-done | bytes 786464 | tf_op jit(solution)/shard_map/ppermute | solution.py:1177
  142.2 8.0 %out_proj.1 = (f32[2,256,1536]{2,1,0:T(8,128)}, bf16[2,256,1536]{2,1,0:T(8,128)(2,1)}) custom-call(s32[1]{0:T(128)} %bitcast.c_ref, bf16[2,256,1536]{2,1,0:T(8,128)(2,1)} %x.5, bf16[4,2,256,384]{3,2,1,0:T(8,128)(2,1)} %copy-done.12, bf16[2,2,256,384]{3,2,1,0:T(8,128)(2,1)S(1)} %collective-permute-done.7.m1, ...), custom_call_target="tpu_custom_call" | custom-call | flops 2415919104 | bytes 12582912 | tf_op jit(solution)/shard_map/out_proj/pallas_call | solution.py:812
  151.3 34.5 %collective-permute-done.17 = bf16[2,256,1536]{2,1,0:T(8,128)(2,1)} collective-permute-done((bf16[2,256,1536]{2,1,0:T(8,128)(2,1)}, bf16[2,256,1536]{2,1,0:T(8,128)(2,1)}, u32[]{:S(2)}, u32[]{:S(2)}) %collective-permute-start.17) | collective-permute-done | bytes 1572896 | tf_op jit(solution)/shard_map/ppermute | solution.py:1177
  189.7 4.7 mlp.8
  195.4 5.6 mlp.9
  202.8 5.0 mlp.10
  209.6 5.0 mlp.12
  216.3 18.1 %mlp_gram.2 = bf16[1536,1536]{1,0:T(8,128)(2,1)} custom-call(bf16[512,1536]{1,0:T(8,128)(2,1)} %bitcast.105, bf16[512,1536]{1,0:T(8,128)(2,1)} %bitcast.21.dy.refs_1_, bf16[512,1536]{1,0:T(8,128)(2,1)} %bitcast.22.dy.refs_2_, bf16[512,1536]{1,0:T(8,128)(2,1)} %bitcast.24.dy.refs_3_, bf16[512,1536]{1,0:T(8,128)(2,1)} %bitcast.16.n2.refs_4_, ...), custom_call_target="tpu_custom_call" | custom-call | flops 9663676416 | bytes 23592960 | tf_op jit(solution)/shard_map/mlp_gram/pallas_call | solution.py:988
  241.2 5.2 mlp.13
  256.1 5.0 mlp.11
  267.1 5.2 mlp.15
  272.4 5.1 sum_nt.11
  279.0 4.5 mlp.14
  285.3 18.0 %mlp_gram.3 = bf16[1536,1536]{1,0:T(8,128)(2,1)} custom-call(bf16[512,1536]{1,0:T(8,128)(2,1)} %bitcast.106, bf16[512,1536]{1,0:T(8,128)(2,1)} %bitcast.21.dy.refs_1_, bf16[512,1536]{1,0:T(8,128)(2,1)} %bitcast.22.dy.refs_2_, bf16[512,1536]{1,0:T(8,128)(2,1)} %bitcast.24.dy.refs_3_, bf16[512,1536]{1,0:T(8,128)(2,1)} %bitcast.16.n2.refs_4_, ...), custom_call_target="tpu_custom_call" | custom-call | flops 9663676416 | bytes 23592960 | tf_op jit(solution)/shard_map/mlp_gram/pallas_call | solution.py:988
  309.6 4.5 sum_nt.10
  317.4 9.5 %out_back.1 = (f32[2,256,1536]{2,1,0:T(8,128)}, bf16[2,256,1536]{2,1,0:T(8,128)(2,1)}, bf16[4,2,256,384]{3,2,1,0:T(8,128)(2,1)}) custom-call(s32[1]{0:T(128)} %bitcast.c_ref, bf16[2,256,1536]{2,1,0:T(8,128)(2,1)} %bitcast.113, bf16[2,256,1536]{2,1,0:T(8,128)(2,1)} %bitcast.26.part_b, f32[2,256,1536]{2,1,0:T(8,128)} %get-tuple-element.69.resid, ...), custom_call_target="tpu_custom_call" | custom-call | flops 2415919104 | bytes 20447232 | tf_op jit(solution)/shard_map/out_back/pallas_call | solution.py:858
  331.8 9.0 %out_gram.1 = bf16[4,2,4,192,384]{4,3,2,1,0:T(8,128)(2,1)S(1)} custom-call(s32[1]{0:T(128)} %bitcast.c_ref, s32[1]{0:T(128)} %bitcast.11.f_ref, bf16[4,2,256,384]{3,2,1,0:T(8,128)(2,1)S(1)} %copy-done.13, bf16[2,2,256,384]{3,2,1,0:T(8,128)(2,1)S(1)} %copy-done.15, bf16[2,2,256,384]{3,2,1,0:T(8,128)(2,1)S(1)} %collective-permute-done.8.m2.m3, ...), custom_call_target="tpu_custom_call" | custom-call | flops 2415919104 | bytes 7864320 | tf_op jit(solution)/shard_map/out_gram/pallas_call | solution.py:1054
  347.8 13.1 %collective-permute-done.26.d23 = bf16[2,2,256,384]{3,2,1,0:T(8,128)(2,1)S(1)} collective-permute-done((bf16[2,2,256,384]{3,2,1,0:T(8,128)(2,1)S(1)}, bf16[2,2,256,384]{3,2,1,0:T(8,128)(2,1)S(1)}, u32[]{:S(2)}, u32[]{:S(2)}) %collective-permute-start.26) | collective-permute-done | bytes 786464 | tf_op jit(solution)/shard_map/ppermute | solution.py:1177
  365.5 31.2 %attend_back.1.right.g = bf16[2048,768]{1,0:T(8,128)(2,1)} custom-call(s32[8]{0:T(128)S(1)} %reshape.151.js_ref, s32[1]{0:T(128)} %bitcast.c_ref, bf16[2048,512]{1,0:T(8,128)(2,1)} %copy-done.67, bf16[2048,256]{1,0:T(8,128)(2,1)S(1)} %copy-done.70, bf16[2048,512]{1,0:T(8,128)(2,1)} %copy-done.68, bf16[4,2,256,384]{3,2,1,0:T(8,128)(2,1)S(1)} %copy-done.13, ...), custom_call_target="tpu_custom_call" | custom-call | flops 20000000000 | bytes 12000000 | tf_op jit(solution)/shard_map/attend_back/pallas_call | solution.py:731
  401.4 5.7 %gram.1 = bf16[1536,768]{1,0:T(8,128)(2,1)S(1)} custom-call(bf16[2048,1536]{1,0:T(8,128)(2,1)S(1)} %copy-done.66, bf16[2048,768]{1,0:T(8,128)(2,1)S(1)} %copy-done.63), custom_call_target="tpu_custom_call" | custom-call | flops 4831838208 | bytes 11796480 | tf_op jit(solution)/shard_map/gram/pallas_call | solution.py:1010
  432.4 14.8 %collective-permute-done.37 = bf16[2,4,192,384]{3,2,1,0:T(8,128)(2,1)} collective-permute-done((bf16[2,4,192,384]{3,2,1,0:T(8,128)(2,1)}, bf16[2,4,192,384]{3,2,1,0:T(8,128)(2,1)}, u32[]{:S(2)}, u32[]{:S(2)}) %collective-permute-start.37) | collective-permute-done | bytes 1179680 | tf_op jit(solution)/shard_map/ppermute | solution.py:1177
  458.3 7.7 %collective-permute-done.38 = bf16[4,192,384]{2,1,0:T(8,128)(2,1)S(1)} collective-permute-done((bf16[4,192,384]{2,1,0:T(8,128)(2,1)S(1)}, bf16[4,192,384]{2,1,0:T(8,128)(2,1)S(1)}, u32[]{:S(2)}, u32[]{:S(2)}) %collective-permute-start.38) | collective-permute-done | bytes 589856 | tf_op jit(solution)/shard_map/ppermute | solution.py:1192
  473.2 13.3 %collective-permute-done.39 = bf16[2,192,384]{2,1,0:T(8,128)(2,1)} collective-permute-done((bf16[2,192,384]{2,1,0:T(8,128)(2,1)}, bf16[2,192,384]{2,1,0:T(8,128)(2,1)}, u32[]{:S(2)}, u32[]{:S(2)}) %collective-permute-start.39) | collective-permute-done | bytes 294944 | tf_op jit(solution)/shard_map/ppermute | solution.py:1192
  504.3 25.3 %collective-permute-done.42.o2 = bf16[192,384]{1,0:T(8,128)(2,1)S(1)} collective-permute-done((bf16[192,384]{1,0:T(8,128)(2,1)S(1)}, bf16[192,384]{1,0:T(8,128)(2,1)S(1)}, u32[]{:S(2)}, u32[]{:S(2)}) %collective-permute-start.42) | collective-permute-done | bytes 147488 | tf_op jit(solution)/shard_map/ppermute | solution.py:1177
  539.8 6.2 %collective-permute-done.35.s2 = bf16[192,896]{1,0:T(8,128)(2,1)S(1)} collective-permute-done((bf16[192,896]{1,0:T(8,128)(2,1)S(1)}, bf16[192,896]{1,0:T(8,128)(2,1)S(1)}, u32[]{:S(2)}, u32[]{:S(2)}) %collective-permute-start.35) | collective-permute-done | bytes 344096 | tf_op jit(solution)/shard_map/ppermute | solution.py:1177
  550.2 6.1 %unpack.1 = (f32[192,1536]{1,0:T(8,128)}, f32[192,768]{1,0:T(8,128)}, f32[192,768]{1,0:T(8,128)}, f32[192,1]{1,0:T(8,128)S(1)}, f32[192,1]{1,0:T(8,128)S(1)}, /*index=5*/f32[192,1536]{1,0:T(8,128)}) custom-call(s32[1]{0:T(128)} %bitcast.c_ref, bf16[192,896]{1,0:T(8,128)(2,1)S(1)} %pad_maximum_fusion.9.s0, bf16[192,896]{1,0:T(8,128)(2,1)S(1)} %collective-permute-done.34.s1, ...), custom_call_target="tpu_custom_call" | custom-call | flops 1000000000 | bytes 10000000 | tf_op jit(solution)/shard_map/unpack/pallas_call | solution.py:1106
  (377 shorter events, 194.6 us)
Async XLA Ops:
  7.2 69.2 %all-gather.4.cloned.1.call-start = ((), (), s32[]{:S(2)}) async-start(), calls=%async_computation.3 | async-start | bytes 2654208 | tf_op jit(solution)/shard_map/all_gather | solution.py:1252
  12.2 175.2 %all-gather.6.cloned.1.call-start = ((), (), s32[]{:S(2)}) async-start(), calls=%async_computation.4 | async-start | bytes 5308416 | tf_op jit(solution)/shard_map/all_gather | solution.py:1272
  13.7 225.2 %all-gather.8.cloned.1.call-start = ((), (), s32[]{:S(2)}) async-start(), calls=%async_computation.5 | async-start | bytes 5308416 | tf_op jit(solution)/shard_map/all_gather | solution.py:1272
  19.5 38.3 %collective-permute-start.9 = (bf16[192,384]{1,0:T(8,128)(2,1)S(1)}, bf16[192,384]{1,0:T(8,128)(2,1)S(1)}, u32[]{:S(2)}, u32[]{:S(2)}) collective-permute-start(bf16[192,384]{1,0:T(8,128)(2,1)S(1)} %get-tuple-element.116), channel_id=1, source_target_pairs={{0,4},{4,0},{8,12},{12,8},{16,20},{20,16},{24,28},{28,24},{1,5},{5... | collective-permute-start | bytes 442376 | tf_op jit(solution)/shard_map/ppermute | solution.py:1192
  20.7 35.3 %collective-permute-start.4 = (bf16[2,256,1536]{2,1,0:T(8,128)(2,1)}, bf16[2,256,1536]{2,1,0:T(8,128)(2,1)}, u32[]{:S(2)}, u32[]{:S(2)}) collective-permute-start(bf16[2,256,1536]{2,1,0:T(8,128)(2,1)} %x.5), channel_id=1, source_target_pairs={{0,2},{1,3},{2,0},{3,1},{4,6},{5,7},{6,4},{7,5},{8,10},{9,11},{10,... | collective-permute-start | bytes 4718600 | tf_op jit(solution)/shard_map/ppermute | solution.py:1177
  23.0 50.8 %collective-permute-start.3 = (bf16[2,256,1536]{2,1,0:T(8,128)(2,1)}, bf16[2,256,1536]{2,1,0:T(8,128)(2,1)}, u32[]{:S(2)}, u32[]{:S(2)}) collective-permute-start(bf16[2,256,1536]{2,1,0:T(8,128)(2,1)} %x.5), channel_id=1, source_target_pairs={{0,1},{1,0},{2,3},{3,2},{4,5},{5,4},{6,7},{7,6},{8,9},{9,8},{10,11... | collective-permute-start | bytes 4718600 | tf_op jit(solution)/shard_map/ppermute | solution.py:1173
  25.3 336.6 %reduce-scatter.4.cloned.1.call-start = ((), (), s32[]{:S(2)}) async-start(), calls=%async_computation.6 | async-start | bytes 5308416 | tf_op jit(solution)/shard_map/reduce_scatter | solution.py:1306
  30.9 28.2 %collective-permute-start.12 = (bf16[2,192,384]{2,1,0:T(8,128)(2,1)S(1)}, bf16[2,192,384]{2,1,0:T(8,128)(2,1)S(1)}, u32[]{:S(2)}, u32[]{:S(2)}) collective-permute-start(bf16[2,192,384]{2,1,0:T(8,128)(2,1)S(1)} %pad_maximum_fusion.10), channel_id=1, source_target_pairs={{0,16},{4,20},{8,24},{12,28},{16,0},{20,4},{24,8},{28,12},{1,17},{... | collective-permute-start | bytes 884744 | tf_op jit(solution)/shard_map/ppermute | solution.py:1192
  33.3 26.4 %collective-permute-start.11 = (bf16[192,384]{1,0:T(8,128)(2,1)S(1)}, bf16[192,384]{1,0:T(8,128)(2,1)S(1)}, u32[]{:S(2)}, u32[]{:S(2)}) collective-permute-start(bf16[192,384]{1,0:T(8,128)(2,1)S(1)} %collective-permute-done.10), channel_id=1, source_target_pairs={{0,4},{4,0},{8,12},{12,8},{16,20},{20,16},{24,28},{28,24},{1,5},{5... | collective-permute-start | bytes 442376 | tf_op jit(solution)/shard_map/ppermute | solution.py:1192
  59.4 35.8 %collective-permute-start.6 = (bf16[2,256,1536]{2,1,0:T(8,128)(2,1)S(1)}, bf16[2,256,1536]{2,1,0:T(8,128)(2,1)}, u32[]{:S(2)}, u32[]{:S(2)}) collective-permute-start(bf16[2,256,1536]{2,1,0:T(8,128)(2,1)S(1)} %copy-done.10), channel_id=1, source_target_pairs={{0,2},{1,3},{2,0},{3,1},{4,6},{5,7},{6,4},{7,5},{8,10},{9,11},{10,... | collective-permute-start | bytes 4718600 | tf_op jit(solution)/shard_map/ppermute | solution.py:1177
  72.6 48.0 %collective-permute-start.15 = (bf16[8,192,384]{2,1,0:T(8,128)(2,1)}, bf16[8,192,384]{2,1,0:T(8,128)(2,1)}, u32[]{:S(2)}, u32[]{:S(2)}) collective-permute-start(bf16[8,192,384]{2,1,0:T(8,128)(2,1)} %slice_dynamic-update-slice_fusion.p0), channel_id=1, source_target_pairs={{0,2},{1,3},{2,0},{3,1},{4,6},{5,7},{6,4},{7,5},{8,10},{9,11},{10,... | collective-permute-start | bytes 3538952 | tf_op jit(solution)/shard_map/ppermute | solution.py:1177
  122.7 19.5 %collective-permute-start.8 = (bf16[2,2,256,384]{3,2,1,0:T(8,128)(2,1)}, bf16[2,2,256,384]{3,2,1,0:T(8,128)(2,1)S(1)}, u32[]{:S(2)}, u32[]{:S(2)}) collective-permute-start(bf16[2,2,256,384]{3,2,1,0:T(8,128)(2,1)} %pad_maximum_fusion.2), channel_id=1, source_target_pairs={{0,2},{1,3},{2,0},{3,1},{4,6},{5,7},{6,4},{7,5},{8,10},{9,11},{10,... | collective-permute-start | bytes 2359304 | tf_op jit(solution)/shard_map/ppermute | solution.py:1177
  150.2 35.6 %collective-permute-start.17 = (bf16[2,256,1536]{2,1,0:T(8,128)(2,1)}, bf16[2,256,1536]{2,1,0:T(8,128)(2,1)}, u32[]{:S(2)}, u32[]{:S(2)}) collective-permute-start(bf16[2,256,1536]{2,1,0:T(8,128)(2,1)} %get-tuple-element.70), channel_id=1, source_target_pairs={{0,2},{1,3},{2,0},{3,1},{4,6},{5,7},{6,4},{7,5},{8,10},{9,11},{10,... | collective-permute-start | bytes 4718600 | tf_op jit(solution)/shard_map/ppermute | solution.py:1177
  150.3 45.1 %collective-permute-start.19 = (bf16[2,256,1536]{2,1,0:T(8,128)(2,1)S(1)}, bf16[2,256,1536]{2,1,0:T(8,128)(2,1)}, u32[]{:S(2)}, u32[]{:S(2)}) collective-permute-start(bf16[2,256,1536]{2,1,0:T(8,128)(2,1)S(1)} %copy-done.10), channel_id=1, source_target_pairs={{0,1},{1,0},{2,3},{3,2},{4,5},{5,4},{6,7},{7,6},{8,9},{9,8},{10,11... | collective-permute-start | bytes 4718600 | tf_op jit(solution)/shard_map/ppermute | solution.py:1173
  151.3 44.1 %collective-permute-start.18 = (bf16[2,256,1536]{2,1,0:T(8,128)(2,1)}, bf16[2,256,1536]{2,1,0:T(8,128)(2,1)}, u32[]{:S(2)}, u32[]{:S(2)}) collective-permute-start(bf16[2,256,1536]{2,1,0:T(8,128)(2,1)} %get-tuple-element.70), channel_id=1, source_target_pairs={{0,1},{1,0},{2,3},{3,2},{4,5},{5,4},{6,7},{7,6},{8,9},{9,8},{10,11... | collective-permute-start | bytes 4718600 | tf_op jit(solution)/shard_map/ppermute | solution.py:1173
  185.8 23.8 %collective-permute-start.20 = (bf16[2,256,1536]{2,1,0:T(8,128)(2,1)}, bf16[2,256,1536]{2,1,0:T(8,128)(2,1)}, u32[]{:S(2)}, u32[]{:S(2)}) collective-permute-start(bf16[2,256,1536]{2,1,0:T(8,128)(2,1)} %collective-permute-done.17), channel_id=1, source_target_pairs={{0,1},{1,0},{2,3},{3,2},{4,5},{5,4},{6,7},{7,6},{8,9},{9,8},{10,11... | collective-permute-start | bytes 4718600 | tf_op jit(solution)/shard_map/ppermute | solution.py:1173
  187.4 22.2 %collective-permute-start.21 = (bf16[2,256,1536]{2,1,0:T(8,128)(2,1)}, bf16[2,256,1536]{2,1,0:T(8,128)(2,1)}, u32[]{:S(2)}, u32[]{:S(2)}) collective-permute-start(bf16[2,256,1536]{2,1,0:T(8,128)(2,1)} %collective-permute-done.6), channel_id=1, source_target_pairs={{0,1},{1,0},{2,3},{3,2},{4,5},{5,4},{6,7},{7,6},{8,9},{9,8},{10,11... | collective-permute-start | bytes 4718600 | tf_op jit(solution)/shard_map/ppermute | solution.py:1173
  234.5 237.6 %reduce-scatter.6.cloned.1.call-start = ((), (), s32[]{:S(2)}) async-start(), calls=%async_computation.7 | async-start | bytes 5308416 | tf_op jit(solution)/shard_map/reduce_scatter | solution.py:1326
  277.6 36.6 %collective-permute-start.23 = (bf16[512,1536]{1,0:T(8,128)(2,1)}, bf16[512,1536]{1,0:T(8,128)(2,1)}, u32[]{:S(2)}, u32[]{:S(2)}) collective-permute-start(bf16[512,1536]{1,0:T(8,128)(2,1)} %sum_nt.11), channel_id=1, source_target_pairs={{0,1},{1,0},{2,3},{3,2},{4,5},{5,4},{6,7},{7,6},{8,9},{9,8},{10,11... | collective-permute-start | bytes 4718600 | tf_op jit(solution)/shard_map/ppermute | solution.py:1173
  277.6 39.8 %collective-permute-start.24 = (bf16[512,1536]{1,0:T(8,128)(2,1)}, bf16[512,1536]{1,0:T(8,128)(2,1)}, u32[]{:S(2)}, u32[]{:S(2)}) collective-permute-start(bf16[512,1536]{1,0:T(8,128)(2,1)} %add_convert_fusion.3), channel_id=1, source_target_pairs={{0,2},{1,3},{2,0},{3,1},{4,6},{5,7},{6,4},{7,5},{8,10},{9,11},{10,... | collective-permute-start | bytes 4718600 | tf_op jit(solution)/shard_map/ppermute | solution.py:1177
  303.3 231.8 %reduce-scatter.8.cloned.1.call-start = ((), (), s32[]{:S(2)}) async-start(), calls=%async_computation.8 | async-start | bytes 2654208 | tf_op jit(solution)/shard_map/reduce_scatter | solution.py:1361
  341.9 19.1 %collective-permute-start.26 = (bf16[2,2,256,384]{3,2,1,0:T(8,128)(2,1)S(1)}, bf16[2,2,256,384]{3,2,1,0:T(8,128)(2,1)S(1)}, u32[]{:S(2)}, u32[]{:S(2)}) collective-permute-start(bf16[2,2,256,384]{3,2,1,0:T(8,128)(2,1)S(1)} %pad_maximum_fusion.4), channel_id=1, source_target_pairs={{0,2},{1,3},{2,0},{3,1},{4,6},{5,7},{6,4},{7,5},{8,10},{9,11},{10,... | collective-permute-start | bytes 2359304 | tf_op jit(solution)/shard_map/ppermute | solution.py:1177
  419.3 27.9 %collective-permute-start.37 = (bf16[2,4,192,384]{3,2,1,0:T(8,128)(2,1)}, bf16[2,4,192,384]{3,2,1,0:T(8,128)(2,1)}, u32[]{:S(2)}, u32[]{:S(2)}) collective-permute-start(bf16[2,4,192,384]{3,2,1,0:T(8,128)(2,1)} %fusion.8), channel_id=1, source_target_pairs={{0,2},{1,3},{2,0},{3,1},{4,6},{5,7},{6,4},{7,5},{8,10},{9,11},{10,... | collective-permute-start | bytes 3538952 | tf_op jit(solution)/shard_map/ppermute | solution.py:1177
  426.4 31.5 %collective-permute-start.32 = (bf16[2,256,1536]{2,1,0:T(8,128)(2,1)S(1)}, bf16[2,256,1536]{2,1,0:T(8,128)(2,1)S(1)}, u32[]{:S(2)}, u32[]{:S(2)}) collective-permute-start(bf16[2,256,1536]{2,1,0:T(8,128)(2,1)S(1)} %slice_bitcast_fusion), channel_id=1, source_target_pairs={{0,1},{1,0},{2,3},{3,2},{4,5},{5,4},{6,7},{7,6},{8,9},{9,8},{10,11... | collective-permute-start | bytes 4718600 | tf_op jit(solution)/shard_map/ppermute | solution.py:1173
  431.1 100.2 %collective-permute-start.33 = (bf16[2,256,1536]{2,1,0:T(8,128)(2,1)}, bf16[2,256,1536]{2,1,0:T(8,128)(2,1)}, u32[]{:S(2)}, u32[]{:S(2)}) collective-permute-start(bf16[2,256,1536]{2,1,0:T(8,128)(2,1)} %fusion.2), channel_id=1, source_target_pairs={{0,2},{1,3},{2,0},{3,1},{4,6},{5,7},{6,4},{7,5},{8,10},{9,11},{10,... | collective-permute-start | bytes 4718600 | tf_op jit(solution)/shard_map/ppermute | solution.py:1177
  453.1 34.8 %collective-permute-start.30 = (bf16[512,1536]{1,0:T(8,128)(2,1)}, bf16[512,1536]{1,0:T(8,128)(2,1)}, u32[]{:S(2)}, u32[]{:S(2)}) collective-permute-start(bf16[512,1536]{1,0:T(8,128)(2,1)} %sum_nt.15), channel_id=1, source_target_pairs={{0,1},{1,0},{2,3},{3,2},{4,5},{5,4},{6,7},{7,6},{8,9},{9,8},{10,11... | collective-permute-start | bytes 4718600 | tf_op jit(solution)/shard_map/ppermute | solution.py:1173
  457.9 79.7 %collective-permute-start.29 = (bf16[512,1536]{1,0:T(8,128)(2,1)}, bf16[512,1536]{1,0:T(8,128)(2,1)}, u32[]{:S(2)}, u32[]{:S(2)}) collective-permute-start(bf16[512,1536]{1,0:T(8,128)(2,1)} %sum_nt.13), channel_id=1, source_target_pairs={{0,1},{1,0},{2,3},{3,2},{4,5},{5,4},{6,7},{7,6},{8,9},{9,8},{10,11... | collective-permute-start | bytes 4718600 | tf_op jit(solution)/shard_map/ppermute | solution.py:1173
  467.1 19.4 %collective-permute-start.39 = (bf16[2,192,384]{2,1,0:T(8,128)(2,1)}, bf16[2,192,384]{2,1,0:T(8,128)(2,1)}, u32[]{:S(2)}, u32[]{:S(2)}) collective-permute-start(bf16[2,192,384]{2,1,0:T(8,128)(2,1)} %slice.213), channel_id=1, source_target_pairs={{0,16},{4,20},{8,24},{12,28},{16,0},{20,4},{24,8},{28,12},{1,17},{... | collective-permute-start | bytes 884744 | tf_op jit(solution)/shard_map/ppermute | solution.py:1192
  491.1 55.7 %collective-permute-start.31 = (bf16[512,1536]{1,0:T(8,128)(2,1)}, bf16[512,1536]{1,0:T(8,128)(2,1)}, u32[]{:S(2)}, u32[]{:S(2)}) collective-permute-start(bf16[512,1536]{1,0:T(8,128)(2,1)} %add_convert_fusion), channel_id=1, source_target_pairs={{0,2},{1,3},{2,0},{3,1},{4,6},{5,7},{6,4},{7,5},{8,10},{9,11},{10,... | collective-permute-start | bytes 4718600 | tf_op jit(solution)/shard_map/ppermute | solution.py:1177
  497.0 32.6 %collective-permute-start.42 = (bf16[192,384]{1,0:T(8,128)(2,1)S(1)}, bf16[192,384]{1,0:T(8,128)(2,1)S(1)}, u32[]{:S(2)}, u32[]{:S(2)}) collective-permute-start(bf16[192,384]{1,0:T(8,128)(2,1)S(1)} %fusion.19.o0), channel_id=1, source_target_pairs={{0,2},{1,3},{2,0},{3,1},{4,6},{5,7},{6,4},{7,5},{8,10},{9,11},{10,... | collective-permute-start | bytes 442376 | tf_op jit(solution)/shard_map/ppermute | solution.py:1177
  502.1 48.1 %collective-permute-start.41 = (bf16[192,384]{1,0:T(8,128)(2,1)S(1)}, bf16[192,384]{1,0:T(8,128)(2,1)}, u32[]{:S(2)}, u32[]{:S(2)}) collective-permute-start(bf16[192,384]{1,0:T(8,128)(2,1)S(1)} %fusion.19.o0), channel_id=1, source_target_pairs={{0,1},{1,0},{2,3},{3,2},{4,5},{5,4},{6,7},{7,6},{8,9},{9,8},{10,11... | collective-permute-start | bytes 442376 | tf_op jit(solution)/shard_map/ppermute | solution.py:1173
  529.6 20.6 %collective-permute-start.43 = (bf16[192,384]{1,0:T(8,128)(2,1)S(1)}, bf16[192,384]{1,0:T(8,128)(2,1)}, u32[]{:S(2)}, u32[]{:S(2)}) collective-permute-start(bf16[192,384]{1,0:T(8,128)(2,1)S(1)} %collective-permute-done.42.o2), channel_id=1, source_target_pairs={{0,1},{1,0},{2,3},{3,2},{4,5},{5,4},{6,7},{7,6},{8,9},{9,8},{10,11... | collective-permute-start | bytes 442376 | tf_op jit(solution)/shard_map/ppermute | solution.py:1173
  (117 other events, 872.4 us)
Sparse Core Ops, SparseCore 0:
  12.3 64.0 all-gather.3
  79.2 78.8 all-gather.5
  160.8 78.0 all-gather.7
  242.4 94.3 reduce-scatter.3
  340.3 95.1 reduce-scatter.5
  438.8 78.3 reduce-scatter.7
